TPU v7x, 256 devices: a whole 4x4x8 slice. The times are simulated.
256 devices in a mesh: rows: 32 (over x, y, core), hst: 8 (over z).
Axes of the slice: x: 4, y: 4, z: 8, core: 2. Of those that a mesh axis runs over, the one named last changes fastest.
Arguments:
- grad_pooled: bfloat16 [16384, 4, 128], P(('rows', 'hst')), may hold values from -6 to 6
- weights: bfloat16 [16384, 4, 40], P(('rows', 'hst')), may hold values from 0.25 to 1.75
- owner: int32 [16384, 4, 40], P(('rows', 'hst')), may hold values from 0 to 255, as said below
- slot: int32 [16384, 4, 40], P(('rows', 'hst')), may hold values from 0 to 2047, as said below
- lengths: int32 [16384, 4], P(('rows', 'hst')), may hold values from 10 to 40
- counts: int32 [256], P(('rows', 'hst')), may hold values from 1024 to 2048, as said below
- table: float32 [524288, 128], P(('rows', 'hst')), may hold values from -0.6 to 0.6
- states: float32 [524288], P(('rows', 'hst')), may hold values from 0.5 to 20
Outputs:
- weight_grad: float32 [16384, 4, 40], P(('rows', 'hst'))
- new_table: float32 [524288, 128], P(('rows', 'hst'))
- new_states: float32 [524288], P(('rows', 'hst'))
Inputs may be any that keep to these rules, and one draw needn't show every extreme that they name: Among the ids of one device's samples, no owner appears more than 96 times, and in every draw some owner appears exactly 96 times among the ids of every device. Each id's slot is below the count of its owner. `counts`: some device's count is 2048.
All inputs are finite; a program needn't handle non-finite values.
Results may differ from a plain program's by a relative error of at most 0.0003.
Values may be sent and summed in bfloat16 or wider, within the bound.
A program may use at most 128 MiB of HBM per device.

v0:
```python
import jax
import jax.numpy as jnp
from jax import lax
from jax.sharding import PartitionSpec as P

learn_rate = 0.1
epsilon_value = 1e-08


def cut_along(value, dim, devices):
    shape = value.shape
    parts = value.reshape(*shape[:dim], devices, shape[dim] // devices, *shape[dim + 1 :])
    return jnp.moveaxis(parts, dim, 0)


def in_order(parts, dim):
    parts = jnp.moveaxis(parts, 0, dim)
    shape = parts.shape
    return parts.reshape(*shape[:dim], shape[dim] * shape[dim + 1], *shape[dim + 2 :])


def exchange_both(value, axis, axes, splits, concats):
    sizes = [lax.axis_size(a) for a in axes]
    parts = cut_along(value, splits[0], sizes[0])
    parts = jnp.moveaxis(cut_along(parts, splits[1] + 1, sizes[1]), 0, 1)
    inside = parts.shape[2:]
    parts = parts.reshape(-1, *inside)
    parts = lax.all_to_all(parts, axis, split_axis=0, concat_axis=0, tiled=True)
    parts = in_order(parts.reshape(*sizes, *inside), concats[0] + 1)
    return in_order(parts, concats[1])


def local(grad_pooled, weights, owner, slot, lengths, counts, table, states):
    n_rows = lax.axis_size("rows")
    n_hst = lax.axis_size("hst")
    devices = n_rows * n_hst
    bags, features, per_bag = weights.shape
    width = grad_pooled.shape[2]
    touched = table.shape[0]
    total_ids = bags * features * per_bag
    group = features * per_bag
    n_bags = bags * features
    capacity = max(2, 12 * total_ids // (5 * devices))
    slots_all = devices * capacity
    live = jnp.arange(per_bag, dtype=jnp.int32)[None, None, :] < lengths[:, :, None]
    scaled = jnp.where(live, weights, jnp.zeros_like(weights)).reshape(-1)
    flat_grad = grad_pooled.reshape(n_bags, width)
    owner_groups = owner.reshape(bags, group)
    onehot = (
        owner_groups[:, :, None] == jnp.arange(devices, dtype=jnp.int32)[None, None, :]
    ).astype(jnp.bfloat16)
    lower = (
        jnp.arange(group, dtype=jnp.int32)[:, None] > jnp.arange(group, dtype=jnp.int32)[None, :]
    ).astype(jnp.bfloat16)
    within = jnp.einsum("ij,bjd->bid", lower, onehot, preferred_element_type=jnp.float32)
    totals = jnp.sum(onehot.astype(jnp.float32), axis=1)
    before = jnp.cumsum(totals, axis=0) - totals
    rank = jnp.sum(onehot.astype(jnp.float32) * (within + before[:, None, :]), axis=-1)
    places = (owner_groups * capacity + rank.astype(jnp.int32)).reshape(-1)
    bag_index = jnp.arange(total_ids, dtype=jnp.int32) // per_bag
    filled = jnp.zeros((slots_all,), jnp.bool_).at[places].set(True)
    send_weight = (
        jnp.zeros((slots_all,), jnp.bfloat16)
        .at[places]
        .set(scaled)
        .reshape(n_rows, n_hst, capacity)
    )
    send_slot = (
        jnp.zeros((slots_all,), jnp.int32)
        .at[places]
        .set(slot.reshape(-1))
        .reshape(n_rows, n_hst, capacity)
    )
    slot_bag = jnp.zeros((slots_all,), jnp.int32).at[places].set(bag_index)
    chosen = jnp.where(filled[:, None], flat_grad[slot_bag], jnp.zeros((), jnp.bfloat16))
    send_grad = chosen.reshape(n_rows, n_hst, capacity, width)
    got_grad, got_weight, got_slot = (
        exchange_both(send_grad, ("rows", "hst"), ("rows", "hst"), (0, 1), (0, 1)),
        exchange_both(send_weight, ("rows", "hst"), ("rows", "hst"), (0, 1), (0, 1)),
        exchange_both(send_slot, ("rows", "hst"), ("rows", "hst"), (0, 1), (0, 1)),
    )
    got_grad = got_grad.reshape(slots_all, width)
    got_weight = got_weight.reshape(-1)
    got_slot = got_slot.reshape(-1)
    grad_wide = got_grad.astype(jnp.float32)
    terms = got_weight.astype(jnp.float32)[:, None] * grad_wide
    row_grad = jnp.zeros((touched, width), jnp.float32).at[got_slot].add(terms)
    products = jnp.sum(grad_wide * table[got_slot], axis=1)
    returned = exchange_both(
        products.reshape(n_rows, n_hst, capacity), ("rows", "hst"), ("rows", "hst"), (0, 1), (0, 1)
    )
    weight_grad = returned.reshape(-1)[places].reshape(weights.shape)
    weight_grad = jnp.where(live, weight_grad, jnp.zeros_like(weight_grad))
    columns = jnp.arange(touched, dtype=jnp.int32)
    summed = states + jnp.mean(row_grad * row_grad, axis=-1)
    updated = table - learn_rate * row_grad / (jnp.sqrt(summed)[:, None] + epsilon_value)
    keep = columns < counts[0]
    new_table = jnp.where(keep[:, None], updated, jnp.zeros_like(updated))
    new_states = jnp.where(keep, summed, jnp.zeros_like(summed))
    return (weight_grad, new_table, new_states)


def solution(mesh):
    return jax.shard_map(
        local,
        mesh=mesh,
        in_specs=(
            P(("rows", "hst"), None, None),
            P(("rows", "hst"), None, None),
            P(("rows", "hst"), None, None),
            P(("rows", "hst"), None, None),
            P(("rows", "hst"), None),
            P(("rows", "hst")),
            P(("rows", "hst"), None),
            P(("rows", "hst")),
        ),
        out_specs=(P(("rows", "hst"), None, None), P(("rows", "hst"), None), P(("rows", "hst"))),
        check_vma=False,
    )
```

profile of v0, /device:TPU:1, one launch (start us, length us, event | category | flops | bytes accessed | tf_op | source)
XLA Modules:
  0.0 733.6 jit_solution(6443595910627571252)
XLA Ops:
  0.6 0.9 broadcast_multiply_fusion
  1.6 1.0 copy.20
  2.5 2.8 convert_reduce_fusion
  5.5 9.2 %fusion = f32[64,160]{1,0:T(8,128)S(1)} fusion(f32[64,256]{1,0:T(8,128)S(1)} %sub.16, s32[64,160]{1,0:T(8,128)S(1)} %copy.20), kind=kOutput, calls=%fused_computation.12 | convolution fusion | flops 857226240 | bytes 147456 | tf_op jit(solution)/shard_map/ij,bjd->bid/dot_general | solution.py:55
  15.0 0.2 mul.43
  15.7 70.5 %scatter_custom_fusion.3 = bf16[24576]{0:T(1024)(128)(2,1)S(1)} fusion(s32[10240]{0:T(1024)S(1)} %bitcast.71, bf16[10240]{0:T(1024)(128)(2,1)S(1)} %reshape.227, bf16[]{:T(256)} %constant.10.clone.1), kind=kCustom, calls=%fused_computation.46 | custom fusion | bytes 49154 | tf_op jit(solution)/shard_map/scatter | solution.py:65
  86.3 0.8 reshape_transpose_transpose_reshape_reshape_reshape.13
  87.1 15.6 %all-to-all-start.3 = ((bf16[256,1,1,96]{3,2,1,0:T(2,128)(2,1)}), bf16[256,1,1,96]{3,2,1,0:T(2,128)(2,1)S(1)}, u32[]{:S(2)}, u32[]{:S(2)}) async-start(bf16[256,1,1,96]{3,2,1,0:T(2,128)(2,1)} %reshape_transpose_transpose_reshape_reshape_reshape.13), calls=%async_computation.3 | async-start | bytes 262144 | tf_op jit(solution)/shard_map/all_to_all | solution.py:28
  102.7 38.2 %scatter_custom_fusion.1 = s32[24576]{0:T(1024)S(1)} fusion(s32[10240]{0:T(1024)S(1)} %bitcast.72, s32[10240]{0:T(1024)S(1)} %add_select_fusion, s32[]{:T(128)} %constant.18.clone.1), kind=kCustom, calls=%fused_computation.38 | custom fusion | bytes 98308 | tf_op jit(solution)/shard_map/scatter | solution.py:74
  140.9 43.1 %scatter_custom_fusion = pred[24576]{0:T(1024)(128)(4,1)S(1)} fusion(s32[10240]{0:T(1024)S(1)} %bitcast.73, pred[10240]{0:T(1024)(128)(4,1)S(1)} %broadcast.90, pred[]{:T(512)} %constant.15.clone.1), kind=kCustom, calls=%fused_computation.40 | custom fusion | bytes 24577 | tf_op jit(solution)/shard_map/scatter | solution.py:61
  184.3 0.2 reshape.219
  184.5 38.0 %scatter_custom_fusion.2 = s32[24576]{0:T(1024)S(1)} fusion(s32[10240]{0:T(1024)S(1)} %bitcast.74, s32[10240]{0:T(1024)S(1)} %reshape.219, s32[]{:T(128)} %constant.18.clone.1), kind=kCustom, calls=%fused_computation.36 | custom fusion | bytes 98308 | tf_op jit(solution)/shard_map/scatter | solution.py:71
  222.5 0.7 reshape_transpose_transpose_reshape_reshape_reshape.10
  223.2 85.8 %gather_fusion = bf16[24576,128]{1,0:T(8,128)(2,1)} fusion(bf16[256,128]{1,0:T(8,128)(2,1)S(1)} %bitcast.62, s32[24576]{0:T(1024)S(1)} %fusion.10), kind=kCustom, calls=%fused_computation | custom fusion | bytes 12681216 | tf_op jit(solution)/shard_map/gather | solution.py:75
  309.0 13.7 %all-to-all-start.1 = ((s32[256,1,1,96]{3,2,1,0:T(1,128)}), s32[256,1,1,96]{3,2,1,0:T(1,128)S(1)}, u32[]{:S(2)}, u32[]{:S(2)}) async-start(s32[256,1,1,96]{3,2,1,0:T(1,128)} %bitcast.11), calls=%async_computation.1 | async-start | bytes 262144 | tf_op jit(solution)/shard_map/all_to_all | solution.py:28
  322.7 6.5 broadcast_select_fusion
  329.2 6.4 all-to-all-done.1
  335.7 8.2 %all-to-all-start = ((bf16[256,1,1,96,128]{4,3,2,1,0:T(8,128)(2,1)}), bf16[256,1,1,96,128]{4,3,2,1,0:T(8,128)(2,1)}, u32[]{:S(2)}, u32[]{:S(2)}) async-start(bf16[256,1,1,96,128]{4,3,2,1,0:T(8,128)(2,1)} %broadcast_select_fusion), calls=%async_computation | async-start | bytes 12582912 | tf_op jit(solution)/shard_map/all_to_all | solution.py:28
  344.8 0.2 reshape_reshape.8
  345.1 81.3 %gather_fusion.1 = f32[24576,128]{1,0:T(8,128)} fusion(f32[2048,128]{1,0:T(8,128)S(1)} %copy-done.1, s32[24576]{0:T(1024)S(1)} %broadcast_clamp_fusion), kind=kCustom, calls=%fused_computation.1 | custom fusion | bytes 25264128 | tf_op jit(solution)/shard_map/gather | solution.py:88
  426.4 59.7 %all-to-all-done = bf16[256,1,1,96,128]{4,3,2,1,0:T(8,128)(2,1)} async-done(((bf16[256,1,1,96,128]{4,3,2,1,0:T(8,128)(2,1)}), bf16[256,1,1,96,128]{4,3,2,1,0:T(8,128)(2,1)}, u32[]{:S(2)}, u32[]{:S(2)}) %all-to-all-start) | async-done | bytes 6291488 | tf_op jit(solution)/shard_map/all_to_all | solution.py:28
  486.1 10.2 %bitcast_multiply_fusion = f32[24576,128]{1,0:T(8,128)} fusion(f32[24576]{0:T(1024)S(1)} %reshape.170, bf16[32,8,1,96,128]{4,3,1,0,2:T(8,128)(2,1)} %bitcast.33), kind=kLoop, calls=%fused_computation.10 | loop fusion | flops 6291456 | bytes 18972672 | tf_op jit(solution)/shard_map/mul | solution.py:86
  496.3 149.9 %scatter_custom_fusion.4 = f32[2048,128]{1,0:T(8,128)S(1)} fusion(s32[24576]{0:T(1024)S(1)} %bitcast.69, f32[24576,128]{1,0:T(8,128)} %bitcast_multiply_fusion, f32[]{:T(128)} %constant.17.clone.1), kind=kCustom, calls=%fused_computation.21 | custom fusion | flops 3145728 | bytes 1049088 | tf_op jit(solution)/shard_map/scatter-add | solution.py:87
  646.3 0.3 multiply_reduce_fusion.1
  646.6 9.5 %multiply_reduce_fusion = f32[32,8,96]{2,1,0:T(8,128)} fusion(f32[32,8,1,96,128]{4,3,1,0,2:T(8,128)} %bitcast.63, bf16[32,8,1,96,128]{4,3,1,0,2:T(8,128)(2,1)} %bitcast.33), kind=kLoop, calls=%fused_computation.11 | loop fusion | flops 9412608 | bytes 18972672 | tf_op jit(solution)/shard_map/reduce_sum | solution.py:88
  656.1 6.5 all-to-all-start.2
  662.6 0.6 broadcast_select_fusion.1
  663.2 1.5 subtract_select_fusion
  664.7 10.9 %all-to-all-done.2 = f32[256,1,1,96]{3,2,1,0:T(1,128)S(1)} async-done(((f32[256,1,1,96]{3,2,1,0:T(1,128)}), f32[256,1,1,96]{3,2,1,0:T(1,128)S(1)}, u32[]{:S(2)}, u32[]{:S(2)}) %all-to-all-start.2) | async-done | bytes 98336 | tf_op jit(solution)/shard_map/all_to_all | solution.py:28
  675.7 56.8 %gather_fusion.2 = f32[10240]{0:T(1024)S(1)} fusion(f32[24576]{0:T(1024)S(1)} %reshape_reshape.9, s32[10240]{0:T(1024)S(1)} %broadcast_clamp_fusion.1), kind=kCustom, calls=%fused_computation.2 | custom fusion | bytes 122880 | tf_op jit(solution)/shard_map/gather | solution.py:92
  732.5 0.2 reshape.167
  732.9 0.7 copy.26
  (36 shorter events, 1.8 us)
Async XLA Ops:
  0.6 222.6 %copy-start = (bf16[64,4,128]{2,1,0:T(4,128)(2,1)S(1)}, bf16[64,4,128]{2,1,0:T(4,128)(2,1)}, u32[]{:S(2)}) copy-start(bf16[64,4,128]{2,1,0:T(4,128)(2,1)} %param.8) | copy-start | bytes 196612
  5.4 9.7 %copy-start.5 = (s32[64,4]{0,1:T(4,128)S(1)}, s32[64,4]{0,1:T(4,128)}, u32[]{:S(2)}) copy-start(s32[64,4]{0,1:T(4,128)} %param.12) | copy-start | bytes 3076
  5.5 9.8 %copy-start.3 = (bf16[64,4,40]{0,2,1:T(8,128)(2,1)S(1)}, bf16[64,4,40]{0,2,1:T(8,128)(2,1)}, u32[]{:S(2)}) copy-start(bf16[64,4,40]{0,2,1:T(8,128)(2,1)} %param.9) | copy-start | bytes 61444
  5.5 178.7 %copy-start.2 = (s32[64,4,40]{0,2,1:T(8,128)S(1)}, s32[64,4,40]{0,2,1:T(8,128)}, u32[]{:S(2)}) copy-start(s32[64,4,40]{0,2,1:T(8,128)} %param.11) | copy-start | bytes 122884
  87.1 221.9 %all-to-all-start.3 = ((bf16[256,1,1,96]{3,2,1,0:T(2,128)(2,1)}), bf16[256,1,1,96]{3,2,1,0:T(2,128)(2,1)S(1)}, u32[]{:S(2)}, u32[]{:S(2)}) async-start(bf16[256,1,1,96]{3,2,1,0:T(2,128)(2,1)} %reshape_transpose_transpose_reshape_reshape_reshape.13), calls=%async_computation.3 | async-start | bytes 262144 | tf_op jit(solution)/shard_map/all_to_all | solution.py:28
  309.0 26.7 %all-to-all-start.1 = ((s32[256,1,1,96]{3,2,1,0:T(1,128)}), s32[256,1,1,96]{3,2,1,0:T(1,128)S(1)}, u32[]{:S(2)}, u32[]{:S(2)}) async-start(s32[256,1,1,96]{3,2,1,0:T(1,128)} %bitcast.11), calls=%async_computation.1 | async-start | bytes 262144 | tf_op jit(solution)/shard_map/all_to_all | solution.py:28
  322.7 22.4 %copy-start.1 = (f32[2048,128]{1,0:T(8,128)S(1)}, f32[2048,128]{1,0:T(8,128)}, u32[]{:S(2)}) copy-start(f32[2048,128]{1,0:T(8,128)} %param.14) | copy-start | bytes 3145732
  335.7 150.5 %all-to-all-start = ((bf16[256,1,1,96,128]{4,3,2,1,0:T(8,128)(2,1)}), bf16[256,1,1,96,128]{4,3,2,1,0:T(8,128)(2,1)}, u32[]{:S(2)}, u32[]{:S(2)}) async-start(bf16[256,1,1,96,128]{4,3,2,1,0:T(8,128)(2,1)} %broadcast_select_fusion), calls=%async_computation | async-start | bytes 12582912 | tf_op jit(solution)/shard_map/all_to_all | solution.py:28
  496.3 166.3 %copy-start.4 = (f32[2048]{0:T(1024)S(1)}, f32[2048]{0:T(1024)}, u32[]{:S(2)}) copy-start(f32[2048]{0:T(1024)} %param.15) | copy-start | bytes 24580
  656.1 19.5 %all-to-all-start.2 = ((f32[256,1,1,96]{3,2,1,0:T(1,128)}), f32[256,1,1,96]{3,2,1,0:T(1,128)S(1)}, u32[]{:S(2)}, u32[]{:S(2)}) async-start(f32[256,1,1,96]{3,2,1,0:T(1,128)} %bitcast.18), calls=%async_computation.2 | async-start | bytes 262144 | tf_op jit(solution)/shard_map/all_to_all | solution.py:28
where the time goes:
time: 734 us
  local copies, waits for them, and re-layouts  419 us (57%)
  other arithmetic  183 us (25%)
  waiting for transfers between devices  77 us (10%)
  starting transfers between devices  44 us (6%)
  matrix products  9.24 us (1%)
    scatter-add x1, other arithmetic, local(): row_grad = jnp.zeros((touched, width), jnp.float32).at[got_slot].add(terms)  150 us
    gather x1, local copies, waits for them, and re-layouts, local(): flat_grad[slot_bag]  85.8 us
    gather x1, local copies, waits for them, and re-layouts, local(): products = jnp.sum(grad_wide * table[got_slot], axis=1)  81.3 us
    all_to_all x4, waiting for transfers between devices, exchange_both(): parts = lax.all_to_all(parts, axis, split_axis=0, concat_axis=0, tiled=True)  77 us
    scatter x1, local copies, waits for them, and re-layouts, local(): send_weight = jnp.zeros((slots_all,), jnp.bfloat16).at[places].set(scaled...  70.5 us
    gather x1, local copies, waits for them, and re-layouts, local(): weight_grad = returned.reshape(-1)[places].reshape(weights.shape)  56.8 us
    all_to_all x4, starting transfers between devices, exchange_both(): parts = lax.all_to_all(parts, axis, split_axis=0, concat_axis=0, tiled=True)  44 us
    scatter x1, local copies, waits for them, and re-layouts, local(): filled = jnp.zeros((slots_all,), jnp.bool_).at[places].set(True)  43.1 us
  transfers between devices with their start and end apart: 4, of which 3 were waited for; matrix products, arithmetic and copies ran while one was open for 40% of the time, Pallas kernels for 0%

commit v1 on v0

v1 whole, which is shorter than its diff:
```python
import functools
import jax
import jax.numpy as jnp
import numpy as np
from jax import lax
from jax.experimental import pallas as pl
from jax.experimental.pallas import tpu as pltpu
from jax.sharding import PartitionSpec as P

learn_rate = 0.1
epsilon_value = 1e-08
CAP = 96
RP = 128
BOTH = ("rows", "hst")
BF = jnp.bfloat16
F32 = jnp.float32
I32 = jnp.int32


def onehot(mask):
    return jnp.where(mask, 1.0, 0.0).astype(BF)


def iota(shape, dim):
    return lax.broadcasted_iota(I32, shape, dim)


def params(*sem):
    return pltpu.CompilerParams(dimension_semantics=sem or None)


def route_kernel(own_ref, slot_ref, bag_ref, w_ref, meta_ref, bags_ref, rank_ref, acc, base, upper):
    steps, k = own_ref.shape
    n = acc.shape[0]
    acc[...] = jnp.zeros_like(acc)
    base[...] = jnp.zeros_like(base)
    upper[...] = onehot(iota((k, k), 0) < iota((k, k), 1))

    def step(i, carry):
        row = pl.ds(i, 1)
        mask = iota((n, k), 0) == own_ref[row, :]
        a = onehot(mask)
        before = jnp.dot(a, upper[...], preferred_element_type=F32)
        start = jnp.concatenate([base[...]] * (k // RP), axis=1)
        rank = jnp.sum(jnp.where(mask, before + start, 0.0), axis=0, keepdims=True)
        base[...] += jnp.dot(a, jnp.ones((k, RP), BF), preferred_element_type=F32)
        rank = rank.astype(I32)
        rank_ref[row, :] = rank
        put = iota((RP, k), 0) == rank
        slot = slot_ref[row, :]
        parts = [
            (slot >> 8).astype(F32),
            (slot & 255).astype(F32),
            bag_ref[row, :].astype(F32),
            w_ref[row, :],
        ]
        b = jnp.concatenate([jnp.where(put, p, 0.0).astype(BF) for p in parts], axis=0)
        acc[...] += lax.dot_general(a, b, (((1,), (1,)), ((), ())), preferred_element_type=F32)
        return carry

    lax.fori_loop(0, steps, step, 0)
    meta_ref[:, 0:RP] = acc[:, 0:RP] * 256.0 + acc[:, RP : 2 * RP]
    bags_ref[...] = acc[:, 2 * RP : 3 * RP].astype(I32)
    meta_ref[:, RP : 2 * RP] = acc[:, 3 * RP : 4 * RP]


def send_kernel(bag_ref, g_ref, out_ref):
    owners = bag_ref.shape[0]
    bags = g_ref.shape[0]
    pieces = [onehot(iota((bags, RP), 0) == bag_ref[i : i + 1, :]) for i in range(owners)]
    pick = jnp.concatenate(pieces, axis=1)
    rows = lax.dot_general(pick, g_ref[...], (((0,), (0,)), ((), ())), preferred_element_type=F32)
    rows = rows.astype(BF)
    for i in range(owners):
        out_ref[i] = rows[i * RP : i * RP + CAP]


def spots(slot, k):
    hi = jnp.broadcast_to((slot >> 4).astype(F32), (16, k)).astype(BF)
    lo = jnp.broadcast_to((slot & 15).astype(F32), (16, k)).astype(BF)
    return hi, lo == iota((16, k), 0).astype(F32).astype(BF)


def tile_of(hi, base, first, count):
    zero = jnp.zeros_like(base)
    return jnp.concatenate(
        [jnp.where(hi == jnp.asarray(first + t, BF), base, zero) for t in range(count)], axis=0
    )


def rows_kernel(live_ref, slot_ref, table_ref, out_ref, tab):
    c = pl.program_id(0)
    touched, width = table_ref.shape
    k = slot_ref.shape[1]

    @pl.when(c == 0)
    def _():
        for m in range(touched // 128):
            t = table_ref[m * 128 : (m + 1) * 128, :].T
            high = t.astype(BF)
            tab[0:width, m * 128 : (m + 1) * 128] = high
            tab[width : 2 * width, m * 128 : (m + 1) * 128] = (t - high.astype(F32)).astype(BF)

    @pl.when(live_ref[c] != 0)
    def _():
        hi, at = spots(slot_ref[pl.ds(c, 1), :], k)
        base = jnp.where(at, jnp.ones((16, k), BF), jnp.zeros((16, k), BF))
        total = jnp.zeros((2 * width, k), F32)
        for m in range(touched // 256):
            s = tile_of(hi, base, 16 * m, 16)
            total += jnp.dot(tab[:, m * 256 : (m + 1) * 256], s, preferred_element_type=F32)
        out_ref[...] = total[0:width] + total[width:]


def owner_kernel(
    live_ref, count_ref, slot_ref, w_ref, rows_ref, g_ref, table_ref, states_ref,
    prod_ref, new_table_ref, new_states_ref, grad,
):
    c = pl.program_id(0)
    touched, width = table_ref.shape
    k = slot_ref.shape[1]

    @pl.when(c == 0)
    def _():
        grad[...] = jnp.zeros_like(grad)
        prod_ref[...] = jnp.zeros_like(prod_ref)

    @pl.when(live_ref[c] != 0)
    def _():
        g = g_ref[...].reshape(k, width)
        row = pl.ds(c, 1)
        hi, at = spots(slot_ref[row, :], k)
        w = jnp.broadcast_to(w_ref[row, :], (16, k)).astype(BF)
        base = jnp.where(at, w, jnp.zeros_like(w))
        for m in range(touched // 256):
            s = tile_of(hi, base, 16 * m, 16)
            grad[m * 256 : (m + 1) * 256, :] += jnp.dot(s, g, preferred_element_type=F32)
        prod_ref[row, :] = jnp.sum(rows_ref[...] * g.astype(F32).T, axis=0, keepdims=True)

    @pl.when(c == pl.num_programs(0) - 1)
    def _():
        eye = iota((128, 128), 0) == iota((128, 128), 1)
        for m in range(touched // 128):
            rows = slice(m * 128, (m + 1) * 128)
            r = grad[rows, :]
            state = jnp.sum(jnp.where(eye, states_ref[m : m + 1, :], 0.0), axis=1, keepdims=True)
            summed = state + jnp.mean(r * r, axis=1, keepdims=True)
            updated = table_ref[rows, :] - learn_rate * r / (jnp.sqrt(summed) + epsilon_value)
            keep = iota((128, 128), 0) + m * 128 < count_ref[0]
            new_table_ref[rows, :] = jnp.where(keep, updated, 0.0)
            new_states_ref[m : m + 1, :] = jnp.sum(
                jnp.where(eye & keep, summed, 0.0), axis=0, keepdims=True
            )


def back_kernel(own_ref, rank_ref, prod_ref, out_ref, parts):
    steps, k = own_ref.shape
    n = prod_ref.shape[0]
    t = prod_ref[...].T
    high = t.astype(BF)
    rest = t - high.astype(F32)
    mid = rest.astype(BF)
    parts[0:RP, :] = high
    parts[RP : 2 * RP, :] = mid
    parts[2 * RP : 3 * RP, :] = (rest - mid.astype(F32)).astype(BF)

    def step(i, carry):
        row = pl.ds(i, 1)
        a = onehot(iota((n, k), 0) == own_ref[row, :])
        x = jnp.dot(parts[...], a, preferred_element_type=F32)
        x = (x[2 * RP :] + x[RP : 2 * RP]) + x[0:RP]
        out_ref[row, :] = jnp.sum(
            jnp.where(iota((RP, k), 0) == rank_ref[row, :], x, 0.0), axis=0, keepdims=True
        )
        return carry

    lax.fori_loop(0, steps, step, 0)


def local(grad_pooled, weights, owner, slot, lengths, counts, table, states):
    devices = lax.axis_size("rows") * lax.axis_size("hst")
    bags, features, per_bag = weights.shape
    width = grad_pooled.shape[2]
    touched = table.shape[0]
    total_ids = bags * features * per_bag
    n_bags = bags * features
    k1 = 256
    steps = total_ids // k1
    vmem = pl.BlockSpec(memory_space=pltpu.VMEM)
    live = jnp.arange(per_bag, dtype=I32)[None, None, :] < lengths[:, :, None]
    own = jnp.where(live, owner, -1).reshape(steps, k1)
    slots = slot.reshape(steps, k1)
    w = weights.astype(F32).reshape(steps, k1)
    bag = jnp.asarray((np.arange(total_ids) // per_bag).reshape(steps, k1), I32)
    g = grad_pooled.reshape(n_bags, width)

    meta, send_bags, rank = pl.pallas_call(
        route_kernel,
        out_shape=(
            jax.ShapeDtypeStruct((devices, 2 * RP), F32),
            jax.ShapeDtypeStruct((devices, RP), I32),
            jax.ShapeDtypeStruct((steps, k1), I32),
        ),
        in_specs=[vmem] * 4,
        out_specs=(vmem,) * 3,
        scratch_shapes=[
            pltpu.VMEM((devices, 4 * RP), F32),
            pltpu.VMEM((devices, RP), F32),
            pltpu.VMEM((k1, k1), BF),
        ],
        name="route",
    )(own, slots, bag, w)
    got_meta = lax.all_to_all(meta, BOTH, split_axis=0, concat_axis=0, tiled=True)

    group = 16
    send = pl.pallas_call(
        send_kernel,
        grid=(devices // group,),
        out_shape=jax.ShapeDtypeStruct((devices, CAP, width), BF),
        in_specs=[
            pl.BlockSpec((group, RP), lambda i: (i, 0)),
            pl.BlockSpec((n_bags, width), lambda i: (0, 0)),
        ],
        out_specs=pl.BlockSpec((group, CAP, width), lambda i: (i, 0, 0)),
        name="send",
    )(send_bags, g)
    got = lax.all_to_all(send, BOTH, split_axis=0, concat_axis=0, tiled=True)

    srcs = 32
    tiles = CAP // 16
    chunks = devices // srcs * tiles
    k2 = srcs * 16

    def by_chunk(v):
        v = v[:, :CAP].reshape(devices // srcs, srcs, tiles, 16)
        return v.transpose(0, 2, 1, 3).reshape(chunks, k2)

    got_slot = by_chunk(got_meta[:, :RP].astype(I32))
    got_w = by_chunk(got_meta[:, RP:])
    active = (jnp.max(got_w, axis=1) > 0.0).astype(I32)
    ids = chunks * k2

    rows_t = pl.pallas_call(
        rows_kernel,
        grid_spec=pltpu.PrefetchScalarGridSpec(
            num_scalar_prefetch=1,
            grid=(chunks,),
            in_specs=[
                pl.BlockSpec((chunks, k2), lambda c, *_: (0, 0)),
                pl.BlockSpec((touched, width), lambda c, *_: (0, 0)),
            ],
            out_specs=pl.BlockSpec((width, k2), lambda c, *_: (0, c)),
            scratch_shapes=[pltpu.VMEM((2 * width, touched), BF)],
        ),
        out_shape=jax.ShapeDtypeStruct((width, ids), F32),
        cost_estimate=pl.CostEstimate(
            flops=4 * ids * touched * width, bytes_accessed=ids * width * 4, transcendentals=0
        ),
        compiler_params=params("arbitrary"),
        name="table_rows",
    )(active, got_slot, table)

    prods, new_table, new_states = pl.pallas_call(
        owner_kernel,
        grid_spec=pltpu.PrefetchScalarGridSpec(
            num_scalar_prefetch=2,
            grid=(chunks,),
            in_specs=[
                pl.BlockSpec((chunks, k2), lambda c, *_: (0, 0)),
                pl.BlockSpec((chunks, k2), lambda c, *_: (0, 0)),
                pl.BlockSpec((width, k2), lambda c, *_: (0, c)),
                pl.BlockSpec((srcs, 16, width), lambda c, *_: (c // tiles, c % tiles, 0)),
                pl.BlockSpec((touched, width), lambda c, *_: (0, 0)),
                pl.BlockSpec((touched // 128, 128), lambda c, *_: (0, 0)),
            ],
            out_specs=(
                pl.BlockSpec((chunks, k2), lambda c, *_: (0, 0)),
                pl.BlockSpec((touched, width), lambda c, *_: (0, 0)),
                pl.BlockSpec((touched // 128, 128), lambda c, *_: (0, 0)),
            ),
            scratch_shapes=[pltpu.VMEM((touched, width), F32)],
        ),
        out_shape=(
            jax.ShapeDtypeStruct((chunks, k2), F32),
            jax.ShapeDtypeStruct((touched, width), F32),
            jax.ShapeDtypeStruct((touched // 128, 128), F32),
        ),
        compiler_params=params("arbitrary"),
        name="owner_step",
    )(active, counts, got_slot, got_w, rows_t, got, table, states.reshape(touched // 128, 128))

    back = prods.reshape(devices // srcs, tiles, srcs, 16).transpose(0, 2, 1, 3).reshape(devices, CAP)
    back = jnp.pad(back, ((0, 0), (0, RP - CAP)))
    returned = lax.all_to_all(back, BOTH, split_axis=0, concat_axis=0, tiled=True)
    weight_grad = pl.pallas_call(
        back_kernel,
        out_shape=jax.ShapeDtypeStruct((steps, k1), F32),
        in_specs=[vmem] * 3,
        out_specs=vmem,
        scratch_shapes=[pltpu.VMEM((3 * RP, devices), BF)],
        name="back",
    )(own, rank, returned)
    return (weight_grad.reshape(weights.shape), new_table, new_states.reshape(-1))


def solution(mesh):
    return jax.shard_map(
        local,
        mesh=mesh,
        in_specs=(
            P(BOTH, None, None),
            P(BOTH, None, None),
            P(BOTH, None, None),
            P(BOTH, None, None),
            P(BOTH, None),
            P(BOTH),
            P(BOTH, None),
            P(BOTH),
        ),
        out_specs=(P(BOTH, None, None), P(BOTH, None), P(BOTH)),
        check_vma=False,
    )
```

time: 734 us -> 295 us (0.40)
  local copies, waits for them, and re-layouts: 419 us -> 13.5 us
  other arithmetic: 183 us -> 1.03 us
  Pallas kernels: 0 us -> 106 us
  waiting for transfers between devices: 77 us -> 114 us
  blocking collectives: 0 us -> 30 us
  starting transfers between devices: 44 us -> 26.5 us
  matrix products: 9.24 us -> 0 us
    gather x3 -> x0, local copies, waits for them, and re-layouts: 224 us -> none  [the longest x1 85.8 us: local(): flat_grad[slot_bag]]
    scatter x4 -> x0, local copies, waits for them, and re-layouts: 190 us -> none  [the longest x1 70.5 us: local(): send_weight = jnp.zeros((slots_all,), jnp.bfloat16).at[places].set(scaled...]
    scatter-add x1 -> x0, other arithmetic: 150 us -> none  [local(): row_grad = jnp.zeros((touched, width), jnp.float32).at[got_slot].add(terms)]
    pallas_call x0 -> x5, Pallas kernels: none -> 106 us  [the longest x1 34.3 us: local(): pl.pallas_call(owner_kernel, grid_spec=pltpu.PrefetchScalarGridSpec(num_s...]
    all_to_all x4 -> x2, waiting for transfers between devices: 77 us -> 114 us  [the longest x1 111 us: local(): got = lax.all_to_all(send, BOTH, split_axis=0, concat_axis=0, tiled=True)]
    all_to_all x0 -> x1, blocking collectives: none -> 30 us  [local(): lax.all_to_all(back, BOTH, split_axis=0, concat_axis=0, tiled=True)]
    all_to_all x4 -> x2, starting transfers between devices: 44 us -> 26.5 us  [the longest x1 15.6 us: local(): lax.all_to_all(meta, BOTH, split_axis=0, concat_axis=0, tiled=True)]
    reduce_sum x3 -> x0, other arithmetic: 12.6 us -> none  [the longest x1 9.49 us: local(): products = jnp.sum(grad_wide * table[got_slot], axis=1)]
  transfers between devices with their start and end apart: 4 -> 2, of which waited for: 3 -> 2; matrix products, arithmetic and copies ran while one was open for 40% -> 1% of each run, Pallas kernels for 0% -> 9%
where the time goes in v1:
time: 295 us; the launch traced here: 293 us
  waiting for transfers between devices  114 us (39%)
  Pallas kernels  106 us (36%)
  blocking collectives  30 us (10%)
  starting transfers between devices  26.5 us (9%)
  local copies, waits for them, and re-layouts  13.5 us (5%)
    all_to_all x1, waiting for transfers between devices, local(): got = lax.all_to_all(send, BOTH, split_axis=0, concat_axis=0, tiled=True)  111 us
    pallas_call x1, Pallas kernels, local(): pl.pallas_call(owner_kernel, grid_spec=pltpu.PrefetchScalarGridSpec(num_s...  34.3 us
    all_to_all x1, blocking collectives, local(): lax.all_to_all(back, BOTH, split_axis=0, concat_axis=0, tiled=True)  30 us
    pallas_call x1, Pallas kernels, local(): pl.pallas_call(rows_kernel, grid_spec=pltpu.PrefetchScalarGridSpec(num_sc...  27 us
    pallas_call x1, Pallas kernels, local(): pl.pallas_call(route_kernel, out_shape=(jax.ShapeDtypeStruct((devices, 2...  22 us
    all_to_all x1, starting transfers between devices, local(): lax.all_to_all(meta, BOTH, split_axis=0, concat_axis=0, tiled=True)  15.6 us
    pallas_call x1, Pallas kernels, local(): pl.pallas_call(send_kernel, grid=(devices // group,), out_shape=jax.Shape...  11.8 us
    pallas_call x1, Pallas kernels, local(): pl.pallas_call(back_kernel, out_shape=jax.ShapeDtypeStruct((steps, k1), F...  11.1 us
  transfers between devices with their start and end apart: 2, of which 2 were waited for; matrix products, arithmetic and copies ran while one was open for 1% of the time, Pallas kernels for 9%

profile of v1, /device:TPU:1, one launch (start us, length us, event | category | flops | bytes accessed | tf_op | source)
XLA Modules:
  0.0 292.9 jit_solution(13883027417139058821)
XLA Ops:
  0.6 0.9 fusion
  1.5 0.1 copy.29
  1.6 0.8 reshape.57.own_ref
  2.4 0.9 copy.31
  3.3 0.8 reshape.72.w_ref
  4.1 1.0 copy.30
  5.1 0.8 reshape.58.slot_ref
  5.8 22.0 %route.1 = (f32[256,256]{1,0:T(8,128)}, s32[256,128]{1,0:T(8,128)}, s32[40,256]{1,0:T(8,128)}) custom-call(s32[40,256]{1,0:T(8,128)} %reshape.57.own_ref, s32[40,256]{1,0:T(8,128)} %reshape.58.slot_ref, s32[40,256]{1,0:T(8,128)} %constant.10.clone.bag_ref, f32[40,256]{1,0:T(8,128)} %reshape.72.w_ref), custom_call_target="tpu_custom_call" | custom-call | tf_op jit(solution)/shard_map/route/pallas_call | solution.py:197
  27.9 1.9 copy.32
  29.8 15.6 %all-to-all-start = ((f32[256,1,256]{2,1,0:T(1,128)}), f32[256,1,256]{2,1,0:T(1,128)S(1)}, u32[]{:S(2)}, u32[]{:S(2)}) async-start(f32[256,1,256]{2,1,0:T(1,128)} %copy.32), calls=%async_computation | async-start | bytes 524288 | tf_op jit(solution)/shard_map/all_to_all | solution.py:213
  45.4 11.8 %send.1 = bf16[256,96,128]{2,1,0:T(8,128)(2,1)} custom-call(s32[256,128]{1,0:T(8,128)} %get-tuple-element.11.bag_ref, bf16[256,128]{1,0:T(8,128)(2,1)} %bitcast.33), custom_call_target="tpu_custom_call" | custom-call | tf_op jit(solution)/shard_map/send/pallas_call | solution.py:216
  57.2 3.8 %all-to-all-done = f32[256,1,256]{2,1,0:T(1,128)S(1)} async-done(((f32[256,1,256]{2,1,0:T(1,128)}), f32[256,1,256]{2,1,0:T(1,128)S(1)}, u32[]{:S(2)}, u32[]{:S(2)}) %all-to-all-start) | async-done | bytes 262176 | tf_op jit(solution)/shard_map/all_to_all | solution.py:213
  61.0 10.8 %all-to-all-start.1 = ((bf16[256,96,128]{2,1,0:T(8,128)(2,1)}), bf16[256,96,128]{2,1,0:T(8,128)(2,1)}, u32[]{:S(2)}, u32[]{:S(2)}) async-start(bf16[256,96,128]{2,1,0:T(8,128)(2,1)} %send.1), calls=%async_computation.1 | async-start | bytes 12582912 | tf_op jit(solution)/shard_map/all_to_all | solution.py:227
  72.8 0.1 reshape.61
  72.9 0.1 bitcast_reduce_fusion
  73.1 0.6 reshape.73.live_ref
  73.7 0.1 reshape.62
  73.8 0.3 copy.36
  74.2 1.0 reshape.63.slot_ref
  75.2 0.3 copy.37
  75.5 1.0 reshape.64.w_ref
  76.6 27.0 %table_rows.1.rows_ref = f32[128,24576]{1,0:T(8,128)} custom-call(s32[48]{0:T(128)} %reshape.73.live_ref, s32[48,512]{1,0:T(8,128)} %reshape.63.slot_ref, f32[2048,128]{1,0:T(8,128)} %table_ref.3), custom_call_target="tpu_custom_call" | custom-call | flops 25769803776 | bytes 12582912 | tf_op jit(solution)/shard_map/table_rows/pallas_call | solution.py:243
  103.5 110.6 %all-to-all-done.1.g_ref = bf16[256,96,128]{2,1,0:T(8,128)(2,1)} async-done(((bf16[256,96,128]{2,1,0:T(8,128)(2,1)}), bf16[256,96,128]{2,1,0:T(8,128)(2,1)}, u32[]{:S(2)}, u32[]{:S(2)}) %all-to-all-start.1) | async-done | bytes 6291488 | tf_op jit(solution)/shard_map/all_to_all | solution.py:227
  214.1 34.3 %owner_step.1 = (f32[48,512]{1,0:T(8,128)}, f32[2048,128]{1,0:T(8,128)}, f32[16,128]{1,0:T(8,128)}) custom-call(s32[48]{0:T(128)} %reshape.73.live_ref, s32[1]{0:T(128)S(6)} %copy.44.count_ref, s32[48,512]{1,0:T(8,128)} %reshape.63.slot_ref, f32[48,512]{1,0:T(8,128)} %reshape.64.w_ref, f32[128,24576]{1,0:T(8,128)} %table_rows.1.rows_ref, ...), custom_call_target="tpu_custom_call" | custom-call | tf_op jit(solution)/shard_map/owner_step/pallas_call | solution.py:263
  248.4 1.2 reshape.67
  249.6 0.3 copy.38
  249.8 0.2 reshape.68
  250.0 0.1 copy.39
  250.1 30.0 %all_to_all.28 = f32[256,1,128]{2,1,0:T(1,128)} all-to-all(f32[256,1,128]{2,1,0:T(1,128)S(1)} %copy.39), channel_id=1, replica_groups=mesh['rows'=32,'hst'=8] {'rows','hst'}, dimensions={0} | all-to-all | bytes 262144 | tf_op jit(solution)/shard_map/all_to_all | solution.py:294
  280.1 11.1 %back.1 = f32[40,256]{1,0:T(8,128)} custom-call(s32[40,256]{1,0:T(8,128)} %reshape.57.own_ref, s32[40,256]{1,0:T(8,128)} %get-tuple-element.9.rank_ref, f32[256,128]{1,0:T(8,128)} %bitcast.31), custom_call_target="tpu_custom_call" | custom-call | tf_op jit(solution)/shard_map/back/pallas_call | solution.py:295
  291.2 1.0 reshape.69
  292.2 0.7 copy.40
  (9 shorter events, 0.3 us)
Async XLA Ops:
  29.8 31.2 %all-to-all-start = ((f32[256,1,256]{2,1,0:T(1,128)}), f32[256,1,256]{2,1,0:T(1,128)S(1)}, u32[]{:S(2)}, u32[]{:S(2)}) async-start(f32[256,1,256]{2,1,0:T(1,128)} %copy.32), calls=%async_computation | async-start | bytes 524288 | tf_op jit(solution)/shard_map/all_to_all | solution.py:213
  61.0 153.1 %all-to-all-start.1 = ((bf16[256,96,128]{2,1,0:T(8,128)(2,1)}), bf16[256,96,128]{2,1,0:T(8,128)(2,1)}, u32[]{:S(2)}, u32[]{:S(2)}) async-start(bf16[256,96,128]{2,1,0:T(8,128)(2,1)} %send.1), calls=%async_computation.1 | async-start | bytes 12582912 | tf_op jit(solution)/shard_map/all_to_all | solution.py:227

commit v2 on v1

v2 whole, which is shorter than its diff:
```python
import functools
import jax
import jax.numpy as jnp
import numpy as np
from jax import lax
from jax.experimental import pallas as pl
from jax.experimental.pallas import tpu as pltpu
from jax.sharding import PartitionSpec as P

learn_rate = 0.1
epsilon_value = 1e-08
CAP = 96
RP = 128
FIELD = 65536
BOTH = ("rows", "hst")
BF = jnp.bfloat16
F32 = jnp.float32
I32 = jnp.int32


def onehot(mask):
    return jnp.where(mask, 1.0, 0.0).astype(BF)


def iota(shape, dim):
    return lax.broadcasted_iota(I32, shape, dim)


def params(*sem):
    return pltpu.CompilerParams(dimension_semantics=sem or None)


def route_kernel(own_ref, slot_ref, bag_ref, w_ref, meta_ref, rank_ref, acc, base, upper):
    steps, k = own_ref.shape
    n = acc.shape[0]
    acc[...] = jnp.zeros_like(acc)
    base[...] = jnp.zeros_like(base)
    upper[...] = onehot(iota((k, k), 0) < iota((k, k), 1))

    def step(i, carry):
        row = pl.ds(i, 1)
        mask = iota((n, k), 0) == own_ref[row, :]
        a = onehot(mask)
        before = jnp.dot(a, upper[...], preferred_element_type=F32)
        start = jnp.concatenate([base[...]] * (k // RP), axis=1)
        rank = jnp.sum(jnp.where(mask, before + start, 0.0), axis=0, keepdims=True)
        base[...] += jnp.dot(a, jnp.ones((k, RP), BF), preferred_element_type=F32)
        rank = rank.astype(I32)
        rank_ref[row, :] = rank
        put = iota((RP, k), 0) == rank
        slot = slot_ref[row, :]
        parts = [
            (slot >> 8).astype(F32),
            (slot & 255).astype(F32),
            bag_ref[row, :].astype(F32),
            w_ref[row, :],
        ]
        b = jnp.concatenate([jnp.where(put, p, 0.0).astype(BF) for p in parts], axis=0)
        acc[...] += lax.dot_general(a, b, (((1,), (1,)), ((), ())), preferred_element_type=F32)
        return carry

    lax.fori_loop(0, steps, step, 0)
    slots = (acc[:, 0:RP] * 256.0 + acc[:, RP : 2 * RP]).astype(I32)
    meta_ref[:, 0, :] = slots * FIELD + acc[:, 2 * RP : 3 * RP].astype(I32)
    meta_ref[:, 1, :] = (acc[:, 3 * RP : 4 * RP] * float(FIELD)).astype(I32)


def spots(slot, k):
    hi = jnp.broadcast_to((slot >> 4).astype(F32), (16, k)).astype(BF)
    lo = jnp.broadcast_to((slot & 15).astype(F32), (16, k)).astype(BF)
    return hi, lo == iota((16, k), 0).astype(F32).astype(BF)


def tile_of(hi, base, first, count):
    zero = jnp.zeros_like(base)
    return jnp.concatenate(
        [jnp.where(hi == jnp.asarray(first + t, BF), base, zero) for t in range(count)], axis=0
    )


def owner_kernel(
    live_ref, count_ref, id_ref, w_ref, g_ref, table_ref, states_ref,
    prod_ref, new_table_ref, new_states_ref, tab, grad, hot,
):
    c = pl.program_id(0)
    touched, width = table_ref.shape
    k = id_ref.shape[2]
    bags = g_ref.shape[2]
    blocks = touched // 128

    @pl.when(c == 0)
    def _():
        grad[...] = jnp.zeros_like(grad)
        for m in range(blocks):
            t = table_ref[m * 128 : (m + 1) * 128, :].T
            high = t.astype(BF)
            tab[0:width, m * 128 : (m + 1) * 128] = high
            tab[width : 2 * width, m * 128 : (m + 1) * 128] = (t - high.astype(F32)).astype(BF)

    prod_ref[...] = jnp.zeros_like(prod_ref)

    def some(q, first, count):
        @pl.when(live_ref[c * 8 + q] != 0)
        def _():
            ids = id_ref[0, pl.ds(q, 1), :]
            per = k // count
            bag = (ids & (FIELD - 1)) + lax.broadcasted_iota(I32, (1, k), 1) // per * bags
            hi, at = spots(bag, k)
            one = jnp.where(at, jnp.ones((16, k), BF), jnp.zeros((16, k), BF))
            got = jnp.zeros((width, k), F32)
            for s in range(count):
                pick = tile_of(hi, one, bags // 16 * s, bags // 16)
                got += jnp.dot(g_ref[first + s], pick, preferred_element_type=F32)
            hi, at = spots(ids >> 16, k)
            w = w_ref[0, pl.ds(q, 1), :].astype(F32) * (1.0 / FIELD)
            w = jnp.broadcast_to(w, (16, k)).astype(BF)
            base = jnp.where(at, w, jnp.zeros_like(w))
            for m in range(touched // 256):
                hot[m * 256 : (m + 1) * 256, :] = tile_of(hi, base, 16 * m, 16)
            rows = jnp.dot(tab[...], hot[...], preferred_element_type=F32)
            rows = rows[0:width] + rows[width:]
            prod_ref[0, pl.ds(q, 1), :] = jnp.sum(rows * got, axis=0, keepdims=True)
            got = got.astype(BF)
            for m in range(touched // 256):
                at = slice(m * 256, (m + 1) * 256)
                grad[:, at] += lax.dot_general(
                    got, hot[at, :], (((1,), (1,)), ((), ())), preferred_element_type=F32
                )

    def low(q, carry):
        some(q, q * 4, 4)
        return carry

    def high_ranks(q, carry):
        some(q, 0, 16)
        return carry

    lax.fori_loop(0, 4, low, 0)
    lax.fori_loop(4, 6, high_ranks, 0)

    @pl.when(c == pl.num_programs(0) - 1)
    def _():
        for m in range(blocks):
            at = slice(m * 128, (m + 1) * 128)
            r = grad[:, at]
            summed = states_ref[m : m + 1, :] + jnp.mean(r * r, axis=0, keepdims=True)
            delta = learn_rate * r / (jnp.sqrt(summed) + epsilon_value)
            left = count_ref[0] - m * 128
            updated = table_ref[at, :] - delta.T
            new_table_ref[at, :] = jnp.where(iota((128, width), 0) < left, updated, 0.0)
            new_states_ref[m : m + 1, :] = jnp.where(iota((1, 128), 1) < left, summed, 0.0)


def back_kernel(own_ref, rank_ref, w_ref, prod_ref, out_ref, parts):
    steps, k = own_ref.shape
    n = prod_ref.shape[0]
    t = prod_ref[...].T
    high = t.astype(BF)
    rest = t - high.astype(F32)
    mid = rest.astype(BF)
    parts[0:RP, :] = high
    parts[RP : 2 * RP, :] = mid
    parts[2 * RP : 3 * RP, :] = (rest - mid.astype(F32)).astype(BF)

    def step(i, carry):
        row = pl.ds(i, 1)
        a = onehot(iota((n, k), 0) == own_ref[row, :])
        x = jnp.dot(parts[...], a, preferred_element_type=F32)
        x = (x[2 * RP :] + x[RP : 2 * RP]) + x[0:RP]
        x = jnp.where(iota((RP, k), 0) == rank_ref[row, :], x, 0.0)
        out_ref[row, :] = jnp.sum(x, axis=0, keepdims=True) / w_ref[row, :]
        return carry

    lax.fori_loop(0, steps, step, 0)


def local(grad_pooled, weights, owner, slot, lengths, counts, table, states):
    devices = lax.axis_size("rows") * lax.axis_size("hst")
    bags, features, per_bag = weights.shape
    width = grad_pooled.shape[2]
    touched = table.shape[0]
    total_ids = bags * features * per_bag
    n_bags = bags * features
    k1 = 256
    steps = total_ids // k1
    vmem = pl.BlockSpec(memory_space=pltpu.VMEM)
    live = jnp.arange(per_bag, dtype=I32)[None, None, :] < lengths[:, :, None]
    own = jnp.where(live, owner, -1).reshape(steps, k1)
    slots = slot.reshape(steps, k1)
    w = weights.astype(F32).reshape(steps, k1)
    bag = jnp.asarray((np.arange(total_ids) // per_bag).reshape(steps, k1), I32)
    g = grad_pooled.reshape(n_bags, width)

    everyone = lax.all_gather(g.T, BOTH, axis=0, tiled=False)
    meta, rank = pl.pallas_call(
        route_kernel,
        out_shape=(
            jax.ShapeDtypeStruct((devices, 2, RP), I32),
            jax.ShapeDtypeStruct((steps, k1), I32),
        ),
        in_specs=[vmem] * 4,
        out_specs=(vmem,) * 2,
        scratch_shapes=[
            pltpu.VMEM((devices, 4 * RP), F32),
            pltpu.VMEM((devices, RP), F32),
            pltpu.VMEM((k1, k1), BF),
        ],
        name="route",
    )(own, slots, bag, w)
    got_meta = lax.all_to_all(meta, BOTH, split_axis=0, concat_axis=0, tiled=True)

    srcs = 16
    groups = devices // srcs
    k2 = 256

    def in_rows(v):
        return jnp.concatenate(
            [
                v[:, 0:64].reshape(groups, 4, k2),
                v[:, 64:80].reshape(groups, 1, k2),
                v[:, 80:96].reshape(groups, 1, k2),
                jnp.zeros((groups, 2, k2), v.dtype),
            ],
            axis=1,
        )

    got_ids = in_rows(got_meta[:, 0, :])
    got_w = in_rows(got_meta[:, 1, :])
    active = (jnp.max(got_w, axis=2) > 0).astype(I32).reshape(-1)

    prods, new_table, new_states = pl.pallas_call(
        owner_kernel,
        grid_spec=pltpu.PrefetchScalarGridSpec(
            num_scalar_prefetch=2,
            grid=(groups,),
            in_specs=[
                pl.BlockSpec((1, 8, k2), lambda c, *_: (c, 0, 0)),
                pl.BlockSpec((1, 8, k2), lambda c, *_: (c, 0, 0)),
                pl.BlockSpec((srcs, width, n_bags), lambda c, *_: (c, 0, 0)),
                pl.BlockSpec((touched, width), lambda c, *_: (0, 0)),
                pl.BlockSpec((touched // 128, 128), lambda c, *_: (0, 0)),
            ],
            out_specs=(
                pl.BlockSpec((1, 8, k2), lambda c, *_: (c, 0, 0)),
                pl.BlockSpec((touched, width), lambda c, *_: (0, 0)),
                pl.BlockSpec((touched // 128, 128), lambda c, *_: (0, 0)),
            ),
            scratch_shapes=[
                pltpu.VMEM((2 * width, touched), BF),
                pltpu.VMEM((width, touched), F32),
                pltpu.VMEM((touched, k2), BF),
            ],
        ),
        out_shape=(
            jax.ShapeDtypeStruct((groups, 8, k2), F32),
            jax.ShapeDtypeStruct((touched, width), F32),
            jax.ShapeDtypeStruct((touched // 128, 128), F32),
        ),
        compiler_params=params("arbitrary"),
        name="owner_step",
    )(active, counts, got_ids, got_w, everyone, table, states.reshape(touched // 128, 128))

    back = jnp.concatenate(
        [
            prods[:, 0:4].reshape(devices, 64),
            prods[:, 4].reshape(devices, 16),
            prods[:, 5].reshape(devices, 16),
        ],
        axis=1,
    )
    back = jnp.pad(back, ((0, 0), (0, RP - CAP)))
    returned = lax.all_to_all(back, BOTH, split_axis=0, concat_axis=0, tiled=True)
    weight_grad = pl.pallas_call(
        back_kernel,
        out_shape=jax.ShapeDtypeStruct((steps, k1), F32),
        in_specs=[vmem] * 4,
        out_specs=vmem,
        scratch_shapes=[pltpu.VMEM((3 * RP, devices), BF)],
        name="back",
    )(own, rank, w, returned)
    return (weight_grad.reshape(weights.shape), new_table, new_states.reshape(-1))


def solution(mesh):
    return jax.shard_map(
        local,
        mesh=mesh,
        in_specs=(
            P(BOTH, None, None),
            P(BOTH, None, None),
            P(BOTH, None, None),
            P(BOTH, None, None),
            P(BOTH, None),
            P(BOTH),
            P(BOTH, None),
            P(BOTH),
        ),
        out_specs=(P(BOTH, None, None), P(BOTH, None), P(BOTH)),
        check_vma=False,
    )
```

time: 295 us -> 264 us (0.89)
  waiting for transfers between devices: 114 us -> 86.7 us
  between operations: 1.44 us -> 14.8 us
  Pallas kernels: 106 us -> 94.7 us
  starting transfers between devices: 26.5 us -> 15.7 us
  blocking collectives: 30 us -> 38.4 us
    all_to_all x1 -> x0, waiting for transfers between devices: 111 us -> none  [local(): got = lax.all_to_all(send, BOTH, split_axis=0, concat_axis=0, tiled=True)]
    all_gather x0 -> x1, waiting for transfers between devices: none -> 71.8 us  [local(): everyone = lax.all_gather(g.T, BOTH, axis=0, tiled=False)]
    pallas_call x3 -> x1, Pallas kernels: 60.8 us -> 22.1 us  [local(): pl.pallas_call(route_kernel, out_shape=(jax.ShapeDtypeStruct((devices, 2,...]
    pallas_call x1, Pallas kernels: 34.3 us -> 61.5 us  [local(): pl.pallas_call(owner_kernel, grid_spec=pltpu.PrefetchScalarGridSpec(num_s...]
    all_to_all x1, waiting for transfers between devices: 3.75 us -> 14.9 us  [local(): lax.all_to_all(meta, BOTH, split_axis=0, concat_axis=0, tiled=True)]
    all_to_all x1 -> x0, starting transfers between devices: 10.8 us -> none  [local(): got = lax.all_to_all(send, BOTH, split_axis=0, concat_axis=0, tiled=True)]
    all_to_all x1, blocking collectives: 30 us -> 38.4 us  [local(): lax.all_to_all(back, BOTH, split_axis=0, concat_axis=0, tiled=True)]
  transfers between devices with their start and end apart: 2 -> 2, of which waited for: 2 -> 2; matrix products, arithmetic and copies ran while one was open for 1% -> 3% of each run, Pallas kernels for 9% -> 8%
where the time goes in v2:
time: 264 us
  Pallas kernels  94.7 us (36%)
  waiting for transfers between devices  86.7 us (33%)
  blocking collectives  38.4 us (15%)
  starting transfers between devices  15.7 us (6%)
  between operations  14.8 us (6%)
  local copies, waits for them, and re-layouts  11.6 us (4%)
    all_gather x1, waiting for transfers between devices, local(): everyone = lax.all_gather(g.T, BOTH, axis=0, tiled=False)  71.8 us
    pallas_call x1, Pallas kernels, local(): pl.pallas_call(owner_kernel, grid_spec=pltpu.PrefetchScalarGridSpec(num_s...  61.5 us
    all_to_all x1, blocking collectives, local(): lax.all_to_all(back, BOTH, split_axis=0, concat_axis=0, tiled=True)  38.4 us
    pallas_call x1, Pallas kernels, local(): pl.pallas_call(route_kernel, out_shape=(jax.ShapeDtypeStruct((devices, 2,...  22.1 us
    all_to_all x1, starting transfers between devices, local(): lax.all_to_all(meta, BOTH, split_axis=0, concat_axis=0, tiled=True)  15.6 us
    all_to_all x1, waiting for transfers between devices, local(): lax.all_to_all(meta, BOTH, split_axis=0, concat_axis=0, tiled=True)  14.9 us
    pallas_call x1, Pallas kernels, local(): pl.pallas_call(back_kernel, out_shape=jax.ShapeDtypeStruct((steps, k1), F...  11.1 us
  transfers between devices with their start and end apart: 2, of which 2 were waited for; matrix products, arithmetic and copies ran while one was open for 3% of the time, Pallas kernels for 8%

profile of v2, /device:TPU:1, one launch (start us, length us, event | category | flops | bytes accessed | tf_op | source)
XLA Modules:
  0.0 263.7 jit_solution(281715207940230388)
XLA Ops:
  7.2 1.6 copy.33
  8.8 0.9 fusion
  9.7 0.1 copy.26
  9.8 0.8 reshape.59.own_ref
  10.6 0.9 copy.28
  11.5 0.8 reshape.75.w_ref
  12.2 1.0 copy.27
  13.2 0.8 reshape.60.slot_ref
  14.0 22.1 %route.1 = (s32[256,2,128]{2,1,0:T(2,128)}, s32[40,256]{1,0:T(8,128)}) custom-call(s32[40,256]{1,0:T(8,128)} %reshape.59.own_ref, s32[40,256]{1,0:T(8,128)} %reshape.60.slot_ref, s32[40,256]{1,0:T(8,128)} %constant.12.clone.bag_ref, f32[40,256]{1,0:T(8,128)} %reshape.75.w_ref), custom_call_target="tpu_custom_call" | custom-call | tf_op jit(solution)/shard_map/route/pallas_call | solution.py:195
  36.1 15.6 %all-to-all-start = ((s32[256,2,128]{2,1,0:T(2,128)}), s32[256,2,128]{2,1,0:T(2,128)S(1)}, u32[]{:S(2)}, u32[]{:S(2)}) async-start(s32[256,2,128]{2,1,0:T(2,128)} %get-tuple-element.9), calls=%async_computation | async-start | bytes 524288 | tf_op jit(solution)/shard_map/all_to_all | solution.py:210
  52.5 14.9 %all-to-all-done = s32[256,2,128]{2,1,0:T(2,128)S(1)} async-done(((s32[256,2,128]{2,1,0:T(2,128)}), s32[256,2,128]{2,1,0:T(2,128)S(1)}, u32[]{:S(2)}, u32[]{:S(2)}) %all-to-all-start) | async-done | bytes 262176 | tf_op jit(solution)/shard_map/all_to_all | solution.py:210
  67.4 0.2 fusion.2
  67.6 0.1 reshape.66
  67.7 0.1 reshape.63
  67.8 0.1 fusion.4
  67.9 0.1 reshape.78
  68.1 0.1 reshape.79
  68.2 0.1 fusion.3
  68.3 0.1 reshape.80
  68.4 0.1 reshape.81
  68.6 0.8 add_add_fusion
  69.3 0.6 reshape.76.live_ref
  69.9 71.8 %all-gather.3.cloned.1.call-done = bf16[32768,256]{1,0:T(8,128)(2,1)} async-done(((bf16[128,256]{1,0:T(8,128)(2,1)}), bf16[32768,256]{1,0:T(8,128)(2,1)}) %all-gather.3.cloned.1.call-update) | async-done | bytes 16777232 | tf_op jit(solution)/shard_map/all_gather | solution.py:194
  141.7 61.5 %owner_step.1 = (f32[16,8,256]{2,1,0:T(8,128)}, f32[2048,128]{1,0:T(8,128)}, f32[16,128]{1,0:T(8,128)}) custom-call(s32[128]{0:T(128)} %reshape.76.live_ref, s32[1]{0:T(128)S(6)} %copy.36.count_ref, s32[16,8,256]{2,1,0:T(8,128)} %get-tuple-element.32.id_ref, s32[16,8,256]{2,1,0:T(8,128)} %get-tuple-element.30.w_ref, bf16[256,128,256]{2,1,0:T(8,128)(2,1)} %bitcast.13, ...), custom_call_target="tpu_custom_call" | custom-call | tf_op jit(solution)/shard_map/owner_step/pallas_call | solution.py:231
  203.1 1.1 slice_reduce_fusion.1
  204.2 0.9 slice.41
  205.1 0.1 reshape.71
  205.4 0.1 select_maximum_fusion
  205.6 38.4 %all_to_all.16 = f32[256,1,128]{2,1,0:T(1,128)} all-to-all(f32[256,1,128]{2,1,0:T(1,128)S(1)} %bitcast.19), channel_id=1, replica_groups=mesh['rows'=32,'hst'=8] {'rows','hst'}, dimensions={0} | all-to-all | bytes 262144 | tf_op jit(solution)/shard_map/all_to_all | solution.py:272
  244.0 11.1 %back.1 = f32[40,256]{1,0:T(8,128)} custom-call(s32[40,256]{1,0:T(8,128)} %reshape.59.own_ref, s32[40,256]{1,0:T(8,128)} %get-tuple-element.8.rank_ref, f32[40,256]{1,0:T(8,128)} %reshape.75.w_ref, f32[256,128]{1,0:T(8,128)} %bitcast.18), custom_call_target="tpu_custom_call" | custom-call | tf_op jit(solution)/shard_map/back/pallas_call | solution.py:273
  255.1 1.0 reshape.72
  256.1 0.7 copy.35
  (7 shorter events, 0.3 us)
Async XLA Ops:
  7.2 134.5 %all-gather.3.cloned.1.call-start = ((), (), s32[]{:S(2)}) async-start(), calls=%async_computation.2 | async-start | bytes 16842752 | tf_op jit(solution)/shard_map/all_gather | solution.py:194
  36.1 31.3 %all-to-all-start = ((s32[256,2,128]{2,1,0:T(2,128)}), s32[256,2,128]{2,1,0:T(2,128)S(1)}, u32[]{:S(2)}, u32[]{:S(2)}) async-start(s32[256,2,128]{2,1,0:T(2,128)} %get-tuple-element.9), calls=%async_computation | async-start | bytes 524288 | tf_op jit(solution)/shard_map/all_to_all | solution.py:210
Sparse Core Ops, SparseCore 0:
  12.1 129.4 all-gather.2

commit v3 on v2

--- a/solution.py
+++ b/solution.py
@@ -30,7 +30,145 @@
     return pltpu.CompilerParams(dimension_semantics=sem or None)
 
 
-def route_kernel(own_ref, slot_ref, bag_ref, w_ref, meta_ref, rank_ref, acc, base, upper):
+MESH = pl.DeviceIdType.MESH
+PARTS = ((0, 32, "xyz"), (32, 48, "yzx"), (80, 48, "zxy"))
+SIZE = {"x": 4, "y": 4, "z": 8}
+STEPS = 8
+
+
+def hops(order):
+    return [(d, s) for d in order for s in range(SIZE[d] // 2)]
+
+
+def copies_count():
+    ring = 2 * STEPS * len(PARTS)
+    return ring, ring + sum(1 + SIZE[order[2]] for _, _, order in PARTS)
+
+
+class Spread:
+    def __init__(self, own, out, send, recv, local):
+        r = lax.axis_index("rows")
+        self.me = {"x": r // 8, "y": (r // 2) % 4, "z": lax.axis_index("hst")}
+        self.c = r % 2
+        self.own, self.out, self.send, self.recv = own, out, send, recv
+        self.used = 0
+        self.started, self.pending = [], {}
+        me = self.me
+        self.local = pltpu.make_async_copy(
+            own,
+            out.at[pl.ds(me["x"], 1), pl.ds(me["y"], 1), pl.ds(self.c, 1), pl.ds(me["z"], 1)],
+            local,
+        )
+
+    def device(self, d=None, by=0, core=None):
+        at = dict(self.me)
+        if d is not None:
+            at[d] = (at[d] + by + SIZE[d]) % SIZE[d]
+        c = self.c if core is None else core
+        return ((at["x"] * 4 + at["y"]) * 2 + c, at["z"])
+
+    def greet(self):
+        barrier = pltpu.get_barrier_semaphore()
+        near = [self.device(d, by) for d in "xyz" for by in (-1, 1)]
+        for to in near + [self.device(core=1 - self.c)]:
+            pl.semaphore_signal(barrier, inc=1, device_id=to, device_id_type=MESH)
+        pl.semaphore_wait(barrier, 7)
+
+    def region(self, part, d, by, half=None):
+        first, count, order = PARTS[part]
+        full = order[: order.index(d)]
+        index = {}
+        for e in "xyz":
+            if e == d:
+                index[e] = pl.ds((self.me[e] + by + SIZE[e]) % SIZE[e], 1)
+            elif e in full:
+                index[e] = pl.ds(0, SIZE[e])
+            else:
+                index[e] = pl.ds(self.me[e], 1)
+        if half is not None:
+            if full:
+                n = SIZE[full[0]] // 2
+                index[full[0]] = pl.ds(half * n, n)
+            else:
+                cut = (count + 31) // 32 * 16
+                first, count = (first, cut) if half == 0 else (first + cut, count - cut)
+        return self.out.at[
+            index["x"], index["y"], pl.ds(self.c, 1), index["z"], pl.ds(first, count), :
+        ]
+
+    def copy(self, ref, to, src=None):
+        i = self.used
+        self.used += 1
+        c = pltpu.make_async_remote_copy(
+            src_ref=ref if src is None else src,
+            dst_ref=ref,
+            send_sem=self.send.at[i],
+            recv_sem=self.recv.at[i],
+            device_id=to,
+            device_id_type=MESH,
+        )
+        c.start()
+        self.started.append(c)
+        return c
+
+    def start(self, part, step, way):
+        d, s = hops(PARTS[part][2])[step]
+        last = s == SIZE[d] // 2 - 1
+        half = None if not last else (0 if way == 1 else 1)
+        ref = self.region(part, d, -way * s, half)
+        first, count, _ = PARTS[part]
+        src = self.own.at[:, :, :, :, pl.ds(first, count), :] if step == 0 else None
+        copy = self.copy(ref, self.device(d, way), src)
+        self.pending[part, way] = (copy, d, -way * (s + 1), half)
+
+    def first(self):
+        for part in range(len(PARTS)):
+            for way in (1, -1):
+                self.start(part, 0, way)
+
+    def give(self, ref):
+        self.given.append(self.copy(ref, self.device(core=1 - self.c)))
+
+    def round(self, step):
+        if step == 0:
+            self.given = []
+        for part, (_, _, order) in enumerate(PARTS):
+            plan = hops(order)
+            d, s = plan[step]
+            more = step + 1 < STEPS
+            same = more and plan[step + 1][0] == d
+            got = []
+            for way in (1, -1):
+                copy, _, by, half = self.pending[part, way]
+                copy.wait_recv()
+                got.append((by, half))
+                if same:
+                    self.start(part, step + 1, way)
+            if more and not same:
+                for way in (1, -1):
+                    self.start(part, step + 1, way)
+                if plan[step + 1][0] == order[2]:
+                    self.give(self.region(part, order[2], 0))
+            if d == order[2]:
+                for by, half in got:
+                    self.give(self.region(part, d, by, half))
+
+    def finish(self):
+        for c in self.given:
+            c.wait_recv()
+        for c in self.started:
+            c.wait_send()
+
+
+def route_kernel(
+    own_ref, slot_ref, bag_ref, w_ref, block_ref,
+    meta_ref, rank_ref, everyone_ref,
+    acc, base, upper, send, recv, placed,
+):
+    spread = Spread(block_ref, everyone_ref, send, recv, placed)
+    spread.greet()
+    spread.local.start()
+    spread.first()
     steps, k = own_ref.shape
     n = acc.shape[0]
     acc[...] = jnp.zeros_like(acc)
@@ -59,10 +197,18 @@
         acc[...] += lax.dot_general(a, b, (((1,), (1,)), ((), ())), preferred_element_type=F32)
         return carry
 
-    lax.fori_loop(0, steps, step, 0)
+    done = 0
+    for i in range(STEPS):
+        upto = (i + 1) * steps // 14 if i < 4 else steps - (STEPS - 1 - i) * steps // 6
+        lax.fori_loop(done, upto, step, 0)
+        done = upto
+        if i == 0:
+            spread.local.wait()
+        spread.round(i)
     slots = (acc[:, 0:RP] * 256.0 + acc[:, RP : 2 * RP]).astype(I32)
     meta_ref[:, 0, :] = slots * FIELD + acc[:, 2 * RP : 3 * RP].astype(I32)
     meta_ref[:, 1, :] = (acc[:, 3 * RP : 4 * RP] * float(FIELD)).astype(I32)
+    spread.finish()
 
 
 def spots(slot, k):
@@ -191,22 +337,28 @@
     bag = jnp.asarray((np.arange(total_ids) // per_bag).reshape(steps, k1), I32)
     g = grad_pooled.reshape(n_bags, width)
 
-    everyone = lax.all_gather(g.T, BOTH, axis=0, tiled=False)
-    meta, rank = pl.pallas_call(
+    flights = copies_count()[1]
+    meta, rank, everyone = pl.pallas_call(
         route_kernel,
         out_shape=(
             jax.ShapeDtypeStruct((devices, 2, RP), I32),
             jax.ShapeDtypeStruct((steps, k1), I32),
+            jax.ShapeDtypeStruct((4, 4, 2, 8, width, n_bags), BF),
         ),
-        in_specs=[vmem] * 4,
-        out_specs=(vmem,) * 2,
+        in_specs=[vmem] * 5,
+        out_specs=(vmem, vmem, pl.BlockSpec(memory_space=pl.ANY)),
         scratch_shapes=[
             pltpu.VMEM((devices, 4 * RP), F32),
             pltpu.VMEM((devices, RP), F32),
             pltpu.VMEM((k1, k1), BF),
+            pltpu.SemaphoreType.DMA((flights,)),
+            pltpu.SemaphoreType.DMA((flights,)),
+            pltpu.SemaphoreType.DMA,
         ],
+        compiler_params=pltpu.CompilerParams(collective_id=0, has_side_effects=True),
         name="route",
-    )(own, slots, bag, w)
+    )(own, slots, bag, w, g.T.reshape(1, 1, 1, 1, width, n_bags))
+    everyone = everyone.reshape(devices, width, n_bags)
     got_meta = lax.all_to_all(meta, BOTH, split_axis=0, concat_axis=0, tiled=True)
 
     srcs = 16

time: 264 us -> 220 us (0.83)
  waiting for transfers between devices: 86.7 us -> 14.8 us
  Pallas kernels: 94.7 us -> 162 us
  blocking collectives: 38.4 us -> 18.6 us
  between operations: 14.8 us -> 1.42 us
  starting transfers between devices: 15.7 us -> 8.7 us
    all_gather x1 -> x0, waiting for transfers between devices: 71.8 us -> none  [local(): everyone = lax.all_gather(g.T, BOTH, axis=0, tiled=False)]
    pallas_call x1, Pallas kernels: 22.1 us -> 72.9 us  [local(): pl.pallas_call(route_kernel, out_shape=(jax.ShapeDtypeStruct((devices, 2,...]
    all_to_all x1, blocking collectives: 38.4 us -> 18.6 us  [local(): lax.all_to_all(back, BOTH, split_axis=0, concat_axis=0, tiled=True)]
    pallas_call x1, Pallas kernels: 61.5 us -> 77.9 us  [local(): pl.pallas_call(owner_kernel, grid_spec=pltpu.PrefetchScalarGridSpec(num_s...]
    all_to_all x1, starting transfers between devices: 15.6 us -> 8.7 us  [local(): lax.all_to_all(meta, BOTH, split_axis=0, concat_axis=0, tiled=True)]
  transfers between devices with their start and end apart: 2 -> 1, of which waited for: 2 -> 1; matrix products, arithmetic and copies ran while one was open for 3% -> 0% of each run, Pallas kernels for 8% -> 0%
where the time goes in v3:
time: 220 us; the launch traced here: 219 us
  Pallas kernels  162 us (74%)
  blocking collectives  18.6 us (8%)
  waiting for transfers between devices  14.8 us (7%)
  local copies, waits for them, and re-layouts  11.7 us (5%)
  starting transfers between devices  8.7 us (4%)
    pallas_call x1, Pallas kernels, local(): pl.pallas_call(owner_kernel, grid_spec=pltpu.PrefetchScalarGridSpec(num_s...  77.9 us
    pallas_call x1, Pallas kernels, local(): pl.pallas_call(route_kernel, out_shape=(jax.ShapeDtypeStruct((devices, 2,...  72.9 us
    all_to_all x1, blocking collectives, local(): lax.all_to_all(back, BOTH, split_axis=0, concat_axis=0, tiled=True)  18.6 us
    all_to_all x1, waiting for transfers between devices, local(): lax.all_to_all(meta, BOTH, split_axis=0, concat_axis=0, tiled=True)  14.8 us
    pallas_call x1, Pallas kernels, local(): pl.pallas_call(back_kernel, out_shape=jax.ShapeDtypeStruct((steps, k1), F...  11.1 us
    all_to_all x1, starting transfers between devices, local(): lax.all_to_all(meta, BOTH, split_axis=0, concat_axis=0, tiled=True)  8.7 us
  transfers between devices with their start and end apart: 1, of which 1 were waited for; matrix products, arithmetic and copies ran while one was open for 0% of the time, Pallas kernels for 0%

profile of v3, /device:TPU:1, one launch (start us, length us, event | category | flops | bytes accessed | tf_op | source)
XLA Modules:
  0.0 218.9 jit_solution(3737927286320038051)
XLA Ops:
  0.6 1.6 copy.29
  2.2 0.9 fusion
  3.1 0.1 copy.26
  3.2 0.8 reshape.65.own_ref
  4.0 0.9 copy.28
  4.9 0.8 reshape.83.w_ref
  5.6 1.0 copy.27
  6.6 0.8 reshape.66.slot_ref
  7.4 72.9 %route.1 = (s32[256,2,128]{2,1,0:T(2,128)}, s32[40,256]{1,0:T(8,128)}, bf16[4,4,2,8,128,256]{5,4,3,2,1,0:T(8,128)(2,1)}) custom-call(s32[40,256]{1,0:T(8,128)} %reshape.65.own_ref, s32[40,256]{1,0:T(8,128)} %reshape.66.slot_ref, s32[40,256]{1,0:T(8,128)} %constant.12.clone.bag_ref, f32[40,256]{1,0:T(8,128)} %reshape.83.w_ref, ...), custom_call_target="tpu_custom_call" | custom-call | tf_op jit(solution)/shard_map/route/pallas_call | solution.py:341
  80.4 8.7 %all-to-all-start = ((s32[256,2,128]{2,1,0:T(2,128)}), s32[256,2,128]{2,1,0:T(2,128)S(1)}, u32[]{:S(2)}, u32[]{:S(2)}) async-start(s32[256,2,128]{2,1,0:T(2,128)} %get-tuple-element.10), calls=%async_computation | async-start | bytes 524288 | tf_op jit(solution)/shard_map/all_to_all | solution.py:362
  89.8 14.8 %all-to-all-done = s32[256,2,128]{2,1,0:T(2,128)S(1)} async-done(((s32[256,2,128]{2,1,0:T(2,128)}), s32[256,2,128]{2,1,0:T(2,128)S(1)}, u32[]{:S(2)}, u32[]{:S(2)}) %all-to-all-start) | async-done | bytes 262176 | tf_op jit(solution)/shard_map/all_to_all | solution.py:362
  104.7 0.2 fusion.2
  104.9 0.1 fusion.3
  105.0 0.1 reshape.74
  105.1 0.1 fusion.4
  105.2 0.1 reshape.71
  105.3 0.1 reshape.85
  105.5 0.1 reshape.86
  105.6 0.1 reshape.87
  105.7 0.1 reshape.88
  105.8 0.8 add_add_fusion
  106.6 0.6 reshape.84.live_ref
  107.2 77.9 %owner_step.1 = (f32[16,8,256]{2,1,0:T(8,128)}, f32[2048,128]{1,0:T(8,128)}, f32[16,128]{1,0:T(8,128)}) custom-call(s32[128]{0:T(128)} %reshape.84.live_ref, s32[1]{0:T(128)S(6)} %copy.36.count_ref, s32[16,8,256]{2,1,0:T(8,128)} %get-tuple-element.34.id_ref, s32[16,8,256]{2,1,0:T(8,128)} %get-tuple-element.32.w_ref, bf16[256,128,256]{2,1,0:T(8,128)(2,1)} %bitcast.15, ...), custom_call_target="tpu_custom_call" | custom-call | tf_op jit(solution)/shard_map/owner_step/pallas_call | solution.py:383
  185.1 1.1 slice_reduce_fusion.1
  186.1 0.9 slice.41
  187.1 0.1 reshape.79
  187.2 0.1 reshape_squeeze.6
  187.4 0.1 select_maximum_fusion
  187.5 18.6 %all_to_all.16 = f32[256,1,128]{2,1,0:T(1,128)} all-to-all(f32[256,1,128]{2,1,0:T(1,128)S(1)} %bitcast.21), channel_id=1, replica_groups=mesh['rows'=32,'hst'=8] {'rows','hst'}, dimensions={0} | all-to-all | bytes 262144 | tf_op jit(solution)/shard_map/all_to_all | solution.py:424
  206.1 11.1 %back.1 = f32[40,256]{1,0:T(8,128)} custom-call(s32[40,256]{1,0:T(8,128)} %reshape.65.own_ref, s32[40,256]{1,0:T(8,128)} %get-tuple-element.9.rank_ref, f32[40,256]{1,0:T(8,128)} %reshape.83.w_ref, f32[256,128]{1,0:T(8,128)} %bitcast.20), custom_call_target="tpu_custom_call" | custom-call | tf_op jit(solution)/shard_map/back/pallas_call | solution.py:425
  217.2 1.0 reshape.80
  218.2 0.7 copy.35
  (4 shorter events, 0.2 us)
Async XLA Ops:
  80.4 24.3 %all-to-all-start = ((s32[256,2,128]{2,1,0:T(2,128)}), s32[256,2,128]{2,1,0:T(2,128)S(1)}, u32[]{:S(2)}, u32[]{:S(2)}) async-start(s32[256,2,128]{2,1,0:T(2,128)} %get-tuple-element.10), calls=%async_computation | async-start | bytes 524288 | tf_op jit(solution)/shard_map/all_to_all | solution.py:362

commit v4 on v3

--- a/solution.py
+++ b/solution.py
@@ -31,18 +31,22 @@
 
 
 MESH = pl.DeviceIdType.MESH
-PARTS = ((0, 32, "xyz"), (32, 48, "yzx"), (80, 48, "zxy"))
+PARTS = ((0, 32, "xyz"), (32, 48, "zyx"), (80, 48, "zxy"))
 SIZE = {"x": 4, "y": 4, "z": 8}
-STEPS = 8
-
-
-def hops(order):
-    return [(d, s) for d in order for s in range(SIZE[d] // 2)]
+TURNS = (0, 0, 1, 2, 0, 0, 1, 2, 1, 2, 0, 0, 0, 1, 2, 0, 1, 2)
+WORK = (2, 3, 2, 0, 1, 3, 2, 0, 4, 0, 6, 17, 0, 0, 0, 0, 0, 0)
+
+
+def plan(order):
+    ring = [(d, s) for d in order for s in range(SIZE[d] // 2)]
+    return [("z", None)] + ring[SIZE["z"] // 2 :] if order[0] == "z" else ring
 
 
 def copies_count():
-    ring = 2 * STEPS * len(PARTS)
-    return ring, ring + sum(1 + SIZE[order[2]] for _, _, order in PARTS)
+    total = 0
+    for _, _, order in PARTS:
+        total += sum(SIZE["z"] - 1 if s is None else 2 for _, s in plan(order)) + 1 + SIZE[order[2]]
+    return total
 
 
 class Spread:
@@ -52,7 +56,9 @@
         self.c = r % 2
         self.own, self.out, self.send, self.recv = own, out, send, recv
         self.used = 0
-        self.started, self.pending = [], {}
+        self.started, self.given = [], []
+        self.step = [0] * len(PARTS)
+        self.pending = [None] * len(PARTS)
         me = self.me
         self.local = pltpu.make_async_copy(
             own,
@@ -66,13 +72,6 @@
             at[d] = (at[d] + by + SIZE[d]) % SIZE[d]
         c = self.c if core is None else core
         return ((at["x"] * 4 + at["y"]) * 2 + c, at["z"])
-
-    def greet(self):
-        barrier = pltpu.get_barrier_semaphore()
-        near = [self.device(d, by) for d in "xyz" for by in (-1, 1)]
-        for to in near + [self.device(core=1 - self.c)]:
-            pl.semaphore_signal(barrier, inc=1, device_id=to, device_id_type=MESH)
-        pl.semaphore_wait(barrier, 7)
 
     def region(self, part, d, by, half=None):
         first, count, order = PARTS[part]
@@ -112,46 +111,46 @@
         return c
 
     def start(self, part, step, way):
-        d, s = hops(PARTS[part][2])[step]
-        last = s == SIZE[d] // 2 - 1
-        half = None if not last else (0 if way == 1 else 1)
+        first, count, order = PARTS[part]
+        d, s = plan(order)[step]
+        src = self.own.at[:, :, :, :, pl.ds(first, count), :] if step == 0 else None
+        if s is None:
+            return self.copy(self.region(part, d, 0), self.device(d, way), src), -way, None
+        half = None if s < SIZE[d] // 2 - 1 else (0 if way == 1 else 1)
         ref = self.region(part, d, -way * s, half)
-        first, count, _ = PARTS[part]
-        src = self.own.at[:, :, :, :, pl.ds(first, count), :] if step == 0 else None
-        copy = self.copy(ref, self.device(d, way), src)
-        self.pending[part, way] = (copy, d, -way * (s + 1), half)
+        return self.copy(ref, self.device(d, way), src), -way * (s + 1), half
+
+    def ways(self, part):
+        _, s = plan(PARTS[part][2])[self.step[part]]
+        return range(1, SIZE["z"]) if s is None else (1, -1)
 
     def first(self):
         for part in range(len(PARTS)):
-            for way in (1, -1):
-                self.start(part, 0, way)
+            self.pending[part] = [self.start(part, 0, way) for way in self.ways(part)]
 
     def give(self, ref):
         self.given.append(self.copy(ref, self.device(core=1 - self.c)))
 
-    def round(self, step):
-        if step == 0:
-            self.given = []
-        for part, (_, _, order) in enumerate(PARTS):
-            plan = hops(order)
-            d, s = plan[step]
-            more = step + 1 < STEPS
-            same = more and plan[step + 1][0] == d
-            got = []
-            for way in (1, -1):
-                copy, _, by, half = self.pending[part, way]
-                copy.wait_recv()
-                got.append((by, half))
-                if same:
-                    self.start(part, step + 1, way)
-            if more and not same:
-                for way in (1, -1):
-                    self.start(part, step + 1, way)
-                if plan[step + 1][0] == order[2]:
-                    self.give(self.region(part, order[2], 0))
-            if d == order[2]:
-                for by, half in got:
-                    self.give(self.region(part, d, by, half))
+    def turn(self, part):
+        order = PARTS[part][2]
+        steps = plan(order)
+        step = self.step[part]
+        d, s = steps[step]
+        more = step + 1 < len(steps)
+        same = more and steps[step + 1][0] == d
+        arrived, self.pending[part] = self.pending[part], []
+        self.step[part] += 1
+        for i, (copy, _, _) in enumerate(arrived):
+            copy.wait_recv()
+            if same:
+                self.pending[part].append(self.start(part, step + 1, (1, -1)[i]))
+        if more and not same:
+            self.pending[part] = [self.start(part, step + 1, way) for way in self.ways(part)]
+            if steps[step + 1][0] == order[2]:
+                self.give(self.region(part, order[2], 0))
+        if d == order[2]:
+            for _, by, half in arrived:
+                self.give(self.region(part, d, by, half))
 
     def finish(self):
         for c in self.given:
@@ -160,13 +159,79 @@
             c.wait_send()
 
 
+ROWS, HST = 32, 8
+PEERS = HST - 1 + ROWS - 1
+
+
+def greet_all():
+    r, z = lax.axis_index("rows"), lax.axis_index("hst")
+    barrier = pltpu.get_barrier_semaphore()
+    for k in range(1, HST):
+        pl.semaphore_signal(barrier, inc=1, device_id=(r, (z + k) % HST), device_id_type=MESH)
+
+    def tell(k, carry):
+        pl.semaphore_signal(barrier, inc=1, device_id=((r + k) % ROWS, z), device_id_type=MESH)
+        return carry
+
+    lax.fori_loop(1, ROWS, tell, 0)
+    pl.semaphore_wait(barrier, PEERS)
+
+
+class Exchange:
+    def __init__(self, src, mid, dst, send, recv):
+        self.r, self.z = lax.axis_index("rows"), lax.axis_index("hst")
+        self.src, self.mid, self.dst, self.send, self.recv = src, mid, dst, send, recv
+
+    def down(self, k):
+        return pltpu.make_async_remote_copy(
+            src_ref=self.src.at[:, pl.ds((self.z + k) % HST, 1)],
+            dst_ref=self.mid.at[:, pl.ds(self.z, 1)],
+            send_sem=self.send.at[k - 1],
+            recv_sem=self.recv.at[k - 1],
+            device_id=(self.r, (self.z + k) % HST),
+            device_id_type=MESH,
+        )
+
+    def across(self, k):
+        to = (self.r + k) % ROWS
+        return pltpu.make_async_remote_copy(
+            src_ref=self.mid.at[pl.ds(to, 1)],
+            dst_ref=self.dst.at[pl.ds(self.r, 1)],
+            send_sem=self.send.at[HST - 2 + k],
+            recv_sem=self.recv.at[HST - 2 + k],
+            device_id=(to, self.z),
+            device_id_type=MESH,
+        )
+
+    def each(self, first, last, act):
+        def body(k, carry):
+            act(k)
+            return carry
+
+        lax.fori_loop(first, last, body, 0)
+
+    def begin(self):
+        self.each(1, HST, lambda k: self.down(k).start())
+        self.mid[:, pl.ds(self.z, 1)] = self.src[:, pl.ds(self.z, 1)]
+
+    def turn(self):
+        self.each(1, HST, lambda k: self.down(k).wait_recv())
+        self.each(1, ROWS, lambda k: self.across(k).start())
+        self.dst[pl.ds(self.r, 1)] = self.mid[pl.ds(self.r, 1)]
+
+    def finish(self):
+        self.each(1, ROWS, lambda k: self.across(k).wait_recv())
+        self.each(1, HST, lambda k: self.down(k).wait_send())
+        self.each(1, ROWS, lambda k: self.across(k).wait_send())
+
+
 def route_kernel(
     own_ref, slot_ref, bag_ref, w_ref, block_ref,
-    meta_ref, rank_ref, everyone_ref,
-    acc, base, upper, send, recv, placed,
+    got_ref, rank_ref, everyone_ref,
+    acc, base, upper, meta_ref, mid_ref, send, recv, placed, meta_send, meta_recv,
 ):
+    greet_all()
     spread = Spread(block_ref, everyone_ref, send, recv, placed)
-    spread.greet()
     spread.local.start()
     spread.first()
     steps, k = own_ref.shape
@@ -197,17 +262,26 @@
         acc[...] += lax.dot_general(a, b, (((1,), (1,)), ((), ())), preferred_element_type=F32)
         return carry
 
+    exchange = Exchange(meta_ref, mid_ref, got_ref, meta_send, meta_recv)
     done = 0
-    for i in range(STEPS):
-        upto = (i + 1) * steps // 14 if i < 4 else steps - (STEPS - 1 - i) * steps // 6
-        lax.fori_loop(done, upto, step, 0)
-        done = upto
+    for i, (part, work) in enumerate(zip(TURNS, WORK)):
+        if work:
+            upto = steps if i == 11 else done + work
+            lax.fori_loop(done, upto, step, 0)
+            done = upto
         if i == 0:
             spread.local.wait()
-        spread.round(i)
-    slots = (acc[:, 0:RP] * 256.0 + acc[:, RP : 2 * RP]).astype(I32)
-    meta_ref[:, 0, :] = slots * FIELD + acc[:, 2 * RP : 3 * RP].astype(I32)
-    meta_ref[:, 1, :] = (acc[:, 3 * RP : 4 * RP] * float(FIELD)).astype(I32)
+        if i == 12:
+            slots = (acc[:, 0:RP] * 256.0 + acc[:, RP : 2 * RP]).astype(I32)
+            ids = slots * FIELD + acc[:, 2 * RP : 3 * RP].astype(I32)
+            meta_ref[:, :, 0, :] = ids.reshape(ROWS, HST, RP)
+            codes = (acc[:, 3 * RP : 4 * RP] * float(FIELD)).astype(I32)
+            meta_ref[:, :, 1, :] = codes.reshape(ROWS, HST, RP)
+            exchange.begin()
+        if i == 13:
+            exchange.turn()
+        spread.turn(part)
+    exchange.finish()
     spread.finish()
 
 
@@ -337,11 +411,11 @@
     bag = jnp.asarray((np.arange(total_ids) // per_bag).reshape(steps, k1), I32)
     g = grad_pooled.reshape(n_bags, width)
 
-    flights = copies_count()[1]
-    meta, rank, everyone = pl.pallas_call(
+    flights = copies_count()
+    got_meta, rank, everyone = pl.pallas_call(
         route_kernel,
         out_shape=(
-            jax.ShapeDtypeStruct((devices, 2, RP), I32),
+            jax.ShapeDtypeStruct((ROWS, HST, 2, RP), I32),
             jax.ShapeDtypeStruct((steps, k1), I32),
             jax.ShapeDtypeStruct((4, 4, 2, 8, width, n_bags), BF),
         ),
@@ -351,15 +425,19 @@
             pltpu.VMEM((devices, 4 * RP), F32),
             pltpu.VMEM((devices, RP), F32),
             pltpu.VMEM((k1, k1), BF),
+            pltpu.VMEM((ROWS, HST, 2, RP), I32),
+            pltpu.VMEM((ROWS, HST, 2, RP), I32),
             pltpu.SemaphoreType.DMA((flights,)),
             pltpu.SemaphoreType.DMA((flights,)),
             pltpu.SemaphoreType.DMA,
+            pltpu.SemaphoreType.DMA((PEERS,)),
+            pltpu.SemaphoreType.DMA((PEERS,)),
         ],
         compiler_params=pltpu.CompilerParams(collective_id=0, has_side_effects=True),
         name="route",
     )(own, slots, bag, w, g.T.reshape(1, 1, 1, 1, width, n_bags))
     everyone = everyone.reshape(devices, width, n_bags)
-    got_meta = lax.all_to_all(meta, BOTH, split_axis=0, concat_axis=0, tiled=True)
+    got_meta = got_meta.reshape(devices, 2, RP)
 
     srcs = 16
     groups = devices // srcs

time: 220 us -> 202 us (0.918)
  blocking collectives: 18.6 us -> 38.8 us
  Pallas kernels: 162 us -> 147 us
  waiting for transfers between devices: 14.8 us -> 0 us
  starting transfers between devices: 8.7 us -> 0 us
    all_to_all x1, blocking collectives: 18.6 us -> 38.8 us  [local(): lax.all_to_all(back, BOTH, split_axis=0, concat_axis=0, tiled=True)]
    pallas_call x1, Pallas kernels: 77.9 us -> 61.5 us  [local(): pl.pallas_call(owner_kernel, grid_spec=pltpu.PrefetchScalarGridSpec(num_s...]
    all_to_all x1 -> x0, waiting for transfers between devices: 14.8 us -> none  [local(): lax.all_to_all(meta, BOTH, split_axis=0, concat_axis=0, tiled=True)]
    all_to_all x1 -> x0, starting transfers between devices: 8.7 us -> none  [local(): lax.all_to_all(meta, BOTH, split_axis=0, concat_axis=0, tiled=True)]
  transfers between devices with their start and end apart: 1 -> 0, of which waited for: 1 -> 0; matrix products, arithmetic and copies ran while one was open for 0% -> 0% of each run, Pallas kernels for 0% -> 0%
where the time goes in v4:
time: 202 us
  Pallas kernels  147 us (73%)
  blocking collectives  38.8 us (19%)
  local copies, waits for them, and re-layouts  12.7 us (6%)
    pallas_call x1, Pallas kernels, local(): pl.pallas_call(route_kernel, out_shape=(jax.ShapeDtypeStruct((ROWS, HST,...  74.8 us
    pallas_call x1, Pallas kernels, local(): pl.pallas_call(owner_kernel, grid_spec=pltpu.PrefetchScalarGridSpec(num_s...  61.5 us
    all_to_all x1, blocking collectives, local(): lax.all_to_all(back, BOTH, split_axis=0, concat_axis=0, tiled=True)  38.8 us
    pallas_call x1, Pallas kernels, local(): pl.pallas_call(back_kernel, out_shape=jax.ShapeDtypeStruct((steps, k1), F...  11.1 us

profile of v4, /device:TPU:1, one launch (start us, length us, event | category | flops | bytes accessed | tf_op | source)
XLA Modules:
  0.0 202.1 jit_solution(940285490341126881)
XLA Ops:
  1.3 0.1 pad.15.clone
  1.4 1.6 copy.33
  2.9 0.9 fusion
  3.8 0.1 copy.30
  3.9 0.8 reshape.68.own_ref
  4.7 0.9 copy.32
  5.6 0.8 reshape.87.w_ref
  6.4 1.0 copy.31
  7.4 0.8 reshape.69.slot_ref
  8.1 74.8 %route.1 = (s32[32,8,2,128]{3,2,1,0:T(2,128)}, s32[40,256]{1,0:T(8,128)}, bf16[4,4,2,8,128,256]{5,4,3,2,1,0:T(8,128)(2,1)}) custom-call(s32[40,256]{1,0:T(8,128)} %reshape.68.own_ref, s32[40,256]{1,0:T(8,128)} %reshape.69.slot_ref, s32[40,256]{1,0:T(8,128)} %constant.12.clone.bag_ref, f32[40,256]{1,0:T(8,128)} %reshape.87.w_ref, ...), custom_call_target="tpu_custom_call" | custom-call | tf_op jit(solution)/shard_map/route/pallas_call | solution.py:415
  82.9 1.3 fusion.2
  84.2 0.1 fusion.3
  84.3 0.1 reshape.78
  84.4 0.1 fusion.4
  84.6 0.1 reshape.75
  84.7 0.1 reshape.89
  84.8 0.1 reshape.90
  84.9 0.1 reshape.91
  85.0 0.1 reshape.92
  85.1 0.8 add_add_fusion
  85.9 0.6 reshape.88.live_ref
  86.5 61.5 %owner_step.1 = (f32[16,8,256]{2,1,0:T(8,128)}, f32[2048,128]{1,0:T(8,128)}, f32[16,128]{1,0:T(8,128)}) custom-call(s32[128]{0:T(128)} %reshape.88.live_ref, s32[1]{0:T(128)S(6)} %copy.44.count_ref, s32[16,8,256]{2,1,0:T(8,128)} %get-tuple-element.34.id_ref, s32[16,8,256]{2,1,0:T(8,128)} %get-tuple-element.32.w_ref, bf16[256,128,256]{2,1,0:T(8,128)(2,1)} %bitcast.20, ...), custom_call_target="tpu_custom_call" | custom-call | tf_op jit(solution)/shard_map/owner_step/pallas_call | solution.py:461
  148.0 1.1 slice_reduce_fusion.1
  149.1 0.9 slice.41
  150.0 0.1 reshape.83
  150.1 0.1 reshape_squeeze.6
  150.2 0.1 reshape_squeeze.7
  150.3 0.1 select_maximum_fusion
  150.4 38.8 %all_to_all.11 = f32[256,1,128]{2,1,0:T(1,128)} all-to-all(f32[256,1,128]{2,1,0:T(1,128)S(1)} %bitcast.26), channel_id=1, replica_groups=mesh['rows'=32,'hst'=8] {'rows','hst'}, dimensions={0} | all-to-all | bytes 262144 | tf_op jit(solution)/shard_map/all_to_all | solution.py:502
  189.2 11.1 %back.1 = f32[40,256]{1,0:T(8,128)} custom-call(s32[40,256]{1,0:T(8,128)} %reshape.68.own_ref, s32[40,256]{1,0:T(8,128)} %get-tuple-element.9.rank_ref, f32[40,256]{1,0:T(8,128)} %reshape.87.w_ref, f32[256,128]{1,0:T(8,128)} %bitcast.25), custom_call_target="tpu_custom_call" | custom-call | tf_op jit(solution)/shard_map/back/pallas_call | solution.py:503
  200.3 1.0 reshape.84
  201.3 0.7 copy.41
  (2 shorter events, 0.0 us)

commit v5 on v4

--- a/solution.py
+++ b/solution.py
@@ -319,43 +319,59 @@
 
     prod_ref[...] = jnp.zeros_like(prod_ref)
 
-    def some(q, first, count):
-        @pl.when(live_ref[c * 8 + q] != 0)
-        def _():
-            ids = id_ref[0, pl.ds(q, 1), :]
+    def row_of(ref, q, rows):
+        return jnp.concatenate([ref[0, pl.ds(q + i, 1), :] for i in range(rows)], axis=1)
+
+    def take(q, first, count, rows):
+        wide = rows * k
+        here = hot.at[:, 0:wide]
+        hi, at = spots(row_of(id_ref, q, rows) >> 16, wide)
+        w = row_of(w_ref, q, rows).astype(F32) * (1.0 / FIELD)
+        w = jnp.broadcast_to(w, (16, wide)).astype(BF)
+        base = jnp.where(at, w, jnp.zeros_like(w))
+        for m in range(touched // 256):
+            here[m * 256 : (m + 1) * 256, :] = tile_of(hi, base, 16 * m, 16)
+        rows_at = jnp.dot(tab[...], here[...], preferred_element_type=F32)
+        parts = []
+        for i in range(rows):
             per = k // count
-            bag = (ids & (FIELD - 1)) + lax.broadcasted_iota(I32, (1, k), 1) // per * bags
+            bag = id_ref[0, pl.ds(q + i, 1), :] & (FIELD - 1)
+            bag = bag + lax.broadcasted_iota(I32, (1, k), 1) // per * bags
             hi, at = spots(bag, k)
             one = jnp.where(at, jnp.ones((16, k), BF), jnp.zeros((16, k), BF))
             got = jnp.zeros((width, k), F32)
             for s in range(count):
                 pick = tile_of(hi, one, bags // 16 * s, bags // 16)
-                got += jnp.dot(g_ref[first + s], pick, preferred_element_type=F32)
-            hi, at = spots(ids >> 16, k)
-            w = w_ref[0, pl.ds(q, 1), :].astype(F32) * (1.0 / FIELD)
-            w = jnp.broadcast_to(w, (16, k)).astype(BF)
-            base = jnp.where(at, w, jnp.zeros_like(w))
-            for m in range(touched // 256):
-                hot[m * 256 : (m + 1) * 256, :] = tile_of(hi, base, 16 * m, 16)
-            rows = jnp.dot(tab[...], hot[...], preferred_element_type=F32)
-            rows = rows[0:width] + rows[width:]
-            prod_ref[0, pl.ds(q, 1), :] = jnp.sum(rows * got, axis=0, keepdims=True)
-            got = got.astype(BF)
-            for m in range(touched // 256):
-                at = slice(m * 256, (m + 1) * 256)
-                grad[:, at] += lax.dot_general(
-                    got, hot[at, :], (((1,), (1,)), ((), ())), preferred_element_type=F32
-                )
-
-    def low(q, carry):
-        some(q, q * 4, 4)
+                got += jnp.dot(g_ref[first + i * count + s], pick, preferred_element_type=F32)
+            parts.append(got)
+        got = jnp.concatenate(parts, axis=1)
+        dots = jnp.sum((rows_at[0:width] + rows_at[width:]) * got, axis=0, keepdims=True)
+        for i in range(rows):
+            prod_ref[0, pl.ds(q + i, 1), :] = dots[:, i * k : (i + 1) * k]
+        got = got.astype(BF)
+        for m in range(touched // 256):
+            at = slice(m * 256, (m + 1) * 256)
+            grad[:, at] += lax.dot_general(
+                got, here[at, :], (((1,), (1,)), ((), ())), preferred_element_type=F32
+            )
+
+    def low(i, carry):
+        q = i * 2
+
+        @pl.when(live_ref[c * 8 + q] + live_ref[c * 8 + q + 1] != 0)
+        def _():
+            take(q, q * 4, 4, 2)
+
         return carry
 
     def high_ranks(q, carry):
-        some(q, 0, 16)
+        @pl.when(live_ref[c * 8 + q] != 0)
+        def _():
+            take(q, 0, 16, 1)
+
         return carry
 
-    lax.fori_loop(0, 4, low, 0)
+    lax.fori_loop(0, 2, low, 0)
     lax.fori_loop(4, 6, high_ranks, 0)
 
     @pl.when(c == pl.num_programs(0) - 1)
@@ -376,22 +392,21 @@
     n = prod_ref.shape[0]
     t = prod_ref[...].T
     high = t.astype(BF)
-    rest = t - high.astype(F32)
-    mid = rest.astype(BF)
     parts[0:RP, :] = high
-    parts[RP : 2 * RP, :] = mid
-    parts[2 * RP : 3 * RP, :] = (rest - mid.astype(F32)).astype(BF)
+    parts[RP : 2 * RP, :] = (t - high.astype(F32)).astype(BF)
+    unroll = 4
 
     def step(i, carry):
-        row = pl.ds(i, 1)
-        a = onehot(iota((n, k), 0) == own_ref[row, :])
-        x = jnp.dot(parts[...], a, preferred_element_type=F32)
-        x = (x[2 * RP :] + x[RP : 2 * RP]) + x[0:RP]
-        x = jnp.where(iota((RP, k), 0) == rank_ref[row, :], x, 0.0)
-        out_ref[row, :] = jnp.sum(x, axis=0, keepdims=True) / w_ref[row, :]
+        for j in range(unroll):
+            row = pl.ds(i * unroll + j, 1)
+            hi, at = spots(own_ref[row, :], k)
+            one = jnp.where(at, jnp.ones((16, k), BF), jnp.zeros((16, k), BF))
+            x = jnp.dot(parts[...], tile_of(hi, one, 0, n // 16), preferred_element_type=F32)
+            x = jnp.where(iota((RP, k), 0) == rank_ref[row, :], x[0:RP] + x[RP:], 0.0)
+            out_ref[row, :] = jnp.sum(x, axis=0, keepdims=True) / w_ref[row, :]
         return carry
 
-    lax.fori_loop(0, steps, step, 0)
+    lax.fori_loop(0, steps // unroll, step, 0)
 
 
 def local(grad_pooled, weights, owner, slot, lengths, counts, table, states):
@@ -478,7 +493,7 @@
             scratch_shapes=[
                 pltpu.VMEM((2 * width, touched), BF),
                 pltpu.VMEM((width, touched), F32),
-                pltpu.VMEM((touched, k2), BF),
+                pltpu.VMEM((touched, 2 * k2), BF),
             ],
         ),
         out_shape=(
@@ -505,7 +520,7 @@
         out_shape=jax.ShapeDtypeStruct((steps, k1), F32),
         in_specs=[vmem] * 4,
         out_specs=vmem,
-        scratch_shapes=[pltpu.VMEM((3 * RP, devices), BF)],
+        scratch_shapes=[pltpu.VMEM((2 * RP, devices), BF)],
         name="back",
     )(own, rank, w, returned)
     return (weight_grad.reshape(weights.shape), new_table, new_states.reshape(-1))

time: 202 us -> 191 us (0.946)
  Pallas kernels: 147 us -> 136 us
    pallas_call x1, Pallas kernels: 11.1 us -> 4.92 us  [local(): pl.pallas_call(back_kernel, out_shape=jax.ShapeDtypeStruct((steps, k1), F...]
    pallas_call x1, Pallas kernels: 61.5 us -> 55.8 us  [local(): pl.pallas_call(owner_kernel, grid_spec=pltpu.PrefetchScalarGridSpec(num_s...]
where the time goes in v5:
time: 191 us; the launch traced here: 190 us
  Pallas kernels  136 us (71%)
  blocking collectives  38.9 us (20%)
  local copies, waits for them, and re-layouts  12.7 us (7%)
    pallas_call x1, Pallas kernels, local(): pl.pallas_call(route_kernel, out_shape=(jax.ShapeDtypeStruct((ROWS, HST,...  74.8 us
    pallas_call x1, Pallas kernels, local(): pl.pallas_call(owner_kernel, grid_spec=pltpu.PrefetchScalarGridSpec(num_s...  55.8 us
    all_to_all x1, blocking collectives, local(): lax.all_to_all(back, BOTH, split_axis=0, concat_axis=0, tiled=True)  38.9 us
    pallas_call x1, Pallas kernels, local(): pl.pallas_call(back_kernel, out_shape=jax.ShapeDtypeStruct((steps, k1), F...  4.92 us

profile of v5, /device:TPU:1, one launch (start us, length us, event | category | flops | bytes accessed | tf_op | source)
XLA Modules:
  0.0 190.4 jit_solution(6006310442707496859)
XLA Ops:
  1.3 0.1 pad.15.clone
  1.4 1.6 copy.33
  2.9 0.9 fusion
  3.8 0.1 copy.30
  3.9 0.8 reshape.68.own_ref
  4.7 0.9 copy.32
  5.6 0.8 reshape.87.w_ref
  6.4 1.0 copy.31
  7.4 0.8 reshape.69.slot_ref
  8.1 74.8 %route.1 = (s32[32,8,2,128]{3,2,1,0:T(2,128)}, s32[40,256]{1,0:T(8,128)}, bf16[4,4,2,8,128,256]{5,4,3,2,1,0:T(8,128)(2,1)}) custom-call(s32[40,256]{1,0:T(8,128)} %reshape.68.own_ref, s32[40,256]{1,0:T(8,128)} %reshape.69.slot_ref, s32[40,256]{1,0:T(8,128)} %constant.12.clone.bag_ref, f32[40,256]{1,0:T(8,128)} %reshape.87.w_ref, ...), custom_call_target="tpu_custom_call" | custom-call | tf_op jit(solution)/shard_map/route/pallas_call | solution.py:430
  82.9 1.3 fusion.2
  84.2 0.1 fusion.3
  84.3 0.1 reshape.78
  84.4 0.1 fusion.4
  84.6 0.1 reshape.75
  84.7 0.1 reshape.89
  84.8 0.1 reshape.90
  84.9 0.1 reshape.91
  85.0 0.1 reshape.92
  85.1 0.8 add_add_fusion
  85.9 0.6 reshape.88.live_ref
  86.5 55.8 %owner_step.1 = (f32[16,8,256]{2,1,0:T(8,128)}, f32[2048,128]{1,0:T(8,128)}, f32[16,128]{1,0:T(8,128)}) custom-call(s32[128]{0:T(128)} %reshape.88.live_ref, s32[1]{0:T(128)S(6)} %copy.44.count_ref, s32[16,8,256]{2,1,0:T(8,128)} %get-tuple-element.34.id_ref, s32[16,8,256]{2,1,0:T(8,128)} %get-tuple-element.32.w_ref, bf16[256,128,256]{2,1,0:T(8,128)(2,1)} %bitcast.20, ...), custom_call_target="tpu_custom_call" | custom-call | tf_op jit(solution)/shard_map/owner_step/pallas_call | solution.py:476
  142.4 1.1 slice_reduce_fusion.1
  143.4 0.9 slice.41
  144.4 0.1 reshape.83
  144.5 0.1 reshape_squeeze.6
  144.6 0.1 reshape_squeeze.7
  144.7 0.1 select_maximum_fusion
  144.8 38.9 %all_to_all.11 = f32[256,1,128]{2,1,0:T(1,128)} all-to-all(f32[256,1,128]{2,1,0:T(1,128)S(1)} %bitcast.26), channel_id=1, replica_groups=mesh['rows'=32,'hst'=8] {'rows','hst'}, dimensions={0} | all-to-all | bytes 262144 | tf_op jit(solution)/shard_map/all_to_all | solution.py:517
  183.7 4.9 %back.1 = f32[40,256]{1,0:T(8,128)} custom-call(s32[40,256]{1,0:T(8,128)} %reshape.68.own_ref, s32[40,256]{1,0:T(8,128)} %get-tuple-element.9.rank_ref, f32[40,256]{1,0:T(8,128)} %reshape.87.w_ref, f32[256,128]{1,0:T(8,128)} %bitcast.25), custom_call_target="tpu_custom_call" | custom-call | tf_op jit(solution)/shard_map/back/pallas_call | solution.py:518
  188.7 1.0 reshape.84
  189.7 0.7 copy.41
  (2 shorter events, 0.0 us)

commit v6 on v5

--- a/solution.py
+++ b/solution.py
@@ -12,6 +12,7 @@
 CAP = 96
 RP = 128
 FIELD = 65536
+SLOT_BITS = 11
 BOTH = ("rows", "hst")
 BF = jnp.bfloat16
 F32 = jnp.float32
@@ -226,7 +227,7 @@
 
 
 def route_kernel(
-    own_ref, slot_ref, bag_ref, w_ref, block_ref,
+    key_ref, bag_ref, w_ref, block_ref,
     got_ref, rank_ref, everyone_ref,
     acc, base, upper, meta_ref, mid_ref, send, recv, placed, meta_send, meta_recv,
 ):
@@ -234,7 +235,7 @@
     spread = Spread(block_ref, everyone_ref, send, recv, placed)
     spread.local.start()
     spread.first()
-    steps, k = own_ref.shape
+    steps, k = key_ref.shape
     n = acc.shape[0]
     acc[...] = jnp.zeros_like(acc)
     base[...] = jnp.zeros_like(base)
@@ -242,7 +243,8 @@
 
     def step(i, carry):
         row = pl.ds(i, 1)
-        mask = iota((n, k), 0) == own_ref[row, :]
+        key = key_ref[row, :]
+        mask = iota((n, k), 0) == (key >> SLOT_BITS)
         a = onehot(mask)
         before = jnp.dot(a, upper[...], preferred_element_type=F32)
         start = jnp.concatenate([base[...]] * (k // RP), axis=1)
@@ -251,7 +253,7 @@
         rank = rank.astype(I32)
         rank_ref[row, :] = rank
         put = iota((RP, k), 0) == rank
-        slot = slot_ref[row, :]
+        slot = key & ((1 << SLOT_BITS) - 1)
         parts = [
             (slot >> 8).astype(F32),
             (slot & 255).astype(F32),
@@ -278,7 +280,7 @@
             codes = (acc[:, 3 * RP : 4 * RP] * float(FIELD)).astype(I32)
             meta_ref[:, :, 1, :] = codes.reshape(ROWS, HST, RP)
             exchange.begin()
-        if i == 13:
+        if i == 15:
             exchange.turn()
         spread.turn(part)
     exchange.finish()
@@ -387,8 +389,8 @@
             new_states_ref[m : m + 1, :] = jnp.where(iota((1, 128), 1) < left, summed, 0.0)
 
 
-def back_kernel(own_ref, rank_ref, w_ref, prod_ref, out_ref, parts):
-    steps, k = own_ref.shape
+def back_kernel(key_ref, rank_ref, w_ref, prod_ref, out_ref, parts):
+    steps, k = key_ref.shape
     n = prod_ref.shape[0]
     t = prod_ref[...].T
     high = t.astype(BF)
@@ -399,7 +401,7 @@
     def step(i, carry):
         for j in range(unroll):
             row = pl.ds(i * unroll + j, 1)
-            hi, at = spots(own_ref[row, :], k)
+            hi, at = spots(key_ref[row, :] >> SLOT_BITS, k)
             one = jnp.where(at, jnp.ones((16, k), BF), jnp.zeros((16, k), BF))
             x = jnp.dot(parts[...], tile_of(hi, one, 0, n // 16), preferred_element_type=F32)
             x = jnp.where(iota((RP, k), 0) == rank_ref[row, :], x[0:RP] + x[RP:], 0.0)
@@ -420,8 +422,8 @@
     steps = total_ids // k1
     vmem = pl.BlockSpec(memory_space=pltpu.VMEM)
     live = jnp.arange(per_bag, dtype=I32)[None, None, :] < lengths[:, :, None]
-    own = jnp.where(live, owner, -1).reshape(steps, k1)
-    slots = slot.reshape(steps, k1)
+    assert touched == 1 << SLOT_BITS
+    key = jnp.where(live, owner * touched + slot, -1).reshape(steps, k1)
     w = weights.astype(F32).reshape(steps, k1)
     bag = jnp.asarray((np.arange(total_ids) // per_bag).reshape(steps, k1), I32)
     g = grad_pooled.reshape(n_bags, width)
@@ -434,7 +436,7 @@
             jax.ShapeDtypeStruct((steps, k1), I32),
             jax.ShapeDtypeStruct((4, 4, 2, 8, width, n_bags), BF),
         ),
-        in_specs=[vmem] * 5,
+        in_specs=[vmem] * 4,
         out_specs=(vmem, vmem, pl.BlockSpec(memory_space=pl.ANY)),
         scratch_shapes=[
             pltpu.VMEM((devices, 4 * RP), F32),
@@ -450,7 +452,7 @@
         ],
         compiler_params=pltpu.CompilerParams(collective_id=0, has_side_effects=True),
         name="route",
-    )(own, slots, bag, w, g.T.reshape(1, 1, 1, 1, width, n_bags))
+    )(key, bag, w, g.T.reshape(1, 1, 1, 1, width, n_bags))
     everyone = everyone.reshape(devices, width, n_bags)
     got_meta = got_meta.reshape(devices, 2, RP)
 
@@ -522,7 +524,7 @@
         out_specs=vmem,
         scratch_shapes=[pltpu.VMEM((2 * RP, devices), BF)],
         name="back",
-    )(own, rank, w, returned)
+    )(key, rank, w, returned)
     return (weight_grad.reshape(weights.shape), new_table, new_states.reshape(-1))
 
 

time: 191 us -> 183 us (0.958)
  blocking collectives: 38.9 us -> 20.6 us
  Pallas kernels: 136 us -> 148 us
    all_to_all x1, blocking collectives: 38.9 us -> 20.6 us  [local(): lax.all_to_all(back, BOTH, split_axis=0, concat_axis=0, tiled=True)]
    pallas_call x1, Pallas kernels: 55.8 us -> 73.5 us  [local(): pl.pallas_call(owner_kernel, grid_spec=pltpu.PrefetchScalarGridSpec(num_s...]
    pallas_call x1, Pallas kernels: 74.8 us -> 69.3 us  [local(): pl.pallas_call(route_kernel, out_shape=(jax.ShapeDtypeStruct((ROWS, HST,...]
where the time goes in v6:
time: 183 us
  Pallas kernels  148 us (81%)
  blocking collectives  20.6 us (11%)
  local copies, waits for them, and re-layouts  10.9 us (6%)
  other arithmetic  1.87 us (1%)
    pallas_call x1, Pallas kernels, local(): pl.pallas_call(owner_kernel, grid_spec=pltpu.PrefetchScalarGridSpec(num_s...  73.5 us
    pallas_call x1, Pallas kernels, local(): pl.pallas_call(route_kernel, out_shape=(jax.ShapeDtypeStruct((ROWS, HST,...  69.3 us
    all_to_all x1, blocking collectives, local(): lax.all_to_all(back, BOTH, split_axis=0, concat_axis=0, tiled=True)  20.6 us
    pallas_call x1, Pallas kernels, local(): pl.pallas_call(back_kernel, out_shape=jax.ShapeDtypeStruct((steps, k1), F...  4.93 us

profile of v6, /device:TPU:1, one launch (start us, length us, event | category | flops | bytes accessed | tf_op | source)
XLA Modules:
  0.0 182.6 jit_solution(17905907644760064950)
XLA Ops:
  1.3 0.1 pad.15.clone
  1.4 1.6 copy.30
  2.9 0.9 add_select_fusion
  3.9 0.1 copy.28
  4.0 0.8 reshape.65.key_ref
  4.8 0.9 copy.29
  5.6 0.8 reshape.83.w_ref
  6.4 69.3 %route.1 = (s32[32,8,2,128]{3,2,1,0:T(2,128)}, s32[40,256]{1,0:T(8,128)}, bf16[4,4,2,8,128,256]{5,4,3,2,1,0:T(8,128)(2,1)}) custom-call(s32[40,256]{1,0:T(8,128)} %reshape.65.key_ref, s32[40,256]{1,0:T(8,128)} %constant.14.clone.bag_ref, f32[40,256]{1,0:T(8,128)} %reshape.83.w_ref, bf16[1,1,1,1,128,256]{5,4,3,2,1,0:T(8,128)(2,1)} %bitcast.27), custom_call_target="tpu_custom_call" | custom-call | tf_op jit(solution)/shard_map/route/pallas_call | solution.py:432
  75.8 1.3 fusion.1
  77.0 0.1 fusion.2
  77.2 0.1 reshape.74
  77.3 0.1 fusion.3
  77.4 0.1 reshape.71
  77.5 0.1 reshape.85
  77.6 0.1 reshape.86
  77.7 0.1 reshape.87
  77.9 0.1 reshape.88
  78.0 0.8 add_add_fusion
  78.8 0.6 reshape.84.live_ref
  79.4 73.5 %owner_step.1 = (f32[16,8,256]{2,1,0:T(8,128)}, f32[2048,128]{1,0:T(8,128)}, f32[16,128]{1,0:T(8,128)}) custom-call(s32[128]{0:T(128)} %reshape.84.live_ref, s32[1]{0:T(128)S(6)} %copy.41.count_ref, s32[16,8,256]{2,1,0:T(8,128)} %get-tuple-element.34.id_ref, s32[16,8,256]{2,1,0:T(8,128)} %get-tuple-element.32.w_ref, bf16[256,128,256]{2,1,0:T(8,128)(2,1)} %bitcast.20, ...), custom_call_target="tpu_custom_call" | custom-call | tf_op jit(solution)/shard_map/owner_step/pallas_call | solution.py:478
  152.9 1.1 slice_reduce_fusion.1
  154.0 0.9 slice.41
  154.9 0.1 reshape.79
  155.0 0.1 reshape_squeeze.6
  155.1 0.1 reshape_squeeze.7
  155.2 0.1 select_maximum_fusion
  155.3 20.6 %all_to_all.11 = f32[256,1,128]{2,1,0:T(1,128)} all-to-all(f32[256,1,128]{2,1,0:T(1,128)S(1)} %bitcast.26), channel_id=1, replica_groups=mesh['rows'=32,'hst'=8] {'rows','hst'}, dimensions={0} | all-to-all | bytes 262144 | tf_op jit(solution)/shard_map/all_to_all | solution.py:519
  175.9 4.9 %back.1 = f32[40,256]{1,0:T(8,128)} custom-call(s32[40,256]{1,0:T(8,128)} %reshape.65.key_ref, s32[40,256]{1,0:T(8,128)} %get-tuple-element.9.rank_ref, f32[40,256]{1,0:T(8,128)} %reshape.83.w_ref, f32[256,128]{1,0:T(8,128)} %bitcast.25), custom_call_target="tpu_custom_call" | custom-call | tf_op jit(solution)/shard_map/back/pallas_call | solution.py:520
  180.9 1.0 reshape.80
  181.9 0.7 copy.38
  (2 shorter events, 0.0 us)
